TPU v7x, 32 devices: a whole 2x2x4 slice. The times are simulated.
32 devices in a mesh: facet: 4 (over z), strip: 8 (over y, x, core).
Axes of the slice: x: 2, y: 2, z: 4, core: 2. Of those that a mesh axis runs over, the one named last changes fastest.
Arguments:
- sky_components: bfloat16 [4, 2, 4, 2048, 2048], P('facet', None, None, 'strip'), may hold values from -6 to 6
- scale_kernels: float32 [4, 33], replicated, may hold values from 0.026111647 to 0.26111647
- row_taper: bfloat16 [4, 2048, 512], P('facet'), may hold values from -0.125 to 0.125
- col_taper: bfloat16 [4, 2048, 1024], P('facet'), may hold values from -0.125 to 0.125
- finish_rows: bfloat16 [4, 512, 128], replicated, may hold values from -0.25 to 0.25
- finish_cols: bfloat16 [4, 512, 128], replicated, may hold values from -0.5 to 0.5
- subgrid_owner: int32 [32], replicated, may hold values from 0 to 31, as said below
- block_cell: int32 [2048, 2], P(('facet', 'strip')), may hold values from 0 to 480
- vis_offset: float32 [2048, 2, 128], P(('facet', 'strip')), may hold values from 0 to 31
- block_owner: int32 [2048, 1], P(('facet', 'strip')), may hold values from 0 to 31; in each aligned block of 64 rows (0 to 63, 64 to 127, ...) at most 4 rows name the same one
- observed: float32 [4096, 2, 128], P(('facet', 'strip')), may hold values from -6 to 6
- antenna_pair_index: int32 [4096, 2, 128], P(('facet', 'strip')), may hold values from 0 to 511
- gains: float32 [2, 512], replicated, may hold values from 0.1 to 1.9
Outputs:
- subgrids: bfloat16 [32, 2, 512, 512], P(('facet', 'strip'))
- residual: float32 [4096, 2, 128], P(('facet', 'strip'))
Inputs may be any that keep to these rules, and one draw needn't show every extreme that they name: Every device number appears once; subgrid_owner[a * 8 + b] = rowperm(a) * 8 + colperm(b) for a permutation rowperm of the subgrid rows and a permutation colperm of the subgrid columns. `block_owner`: among the 64 blocks of one device at most 4 share an owner, and some owner takes exactly 4 of them.
All inputs are finite; a program needn't handle non-finite values.
Results may differ from a plain program's by a relative error of at most 0.02.
Values may be sent and summed in bfloat16 or wider, within the bound.
A program may use at most 128 MiB of HBM per device.

v0:
```python
import functools

import jax
import jax.numpy as jnp
from jax import lax
from jax.experimental import pallas as pl
from jax.experimental.pallas import tpu as pltpu
from jax.sharding import PartitionSpec as P

TILE = 32


KERNEL_WIDTH = 1.5


LANES = 128
COL_TILE = 256
MESH = pl.DeviceIdType.MESH


def fill_bands(taps_ref, across_ref, down_ref, width):
    scales, taps = taps_ref.shape
    span = LANES + taps - 1
    k = lax.broadcasted_iota(jnp.int32, (span, LANES), 0)
    n = lax.broadcasted_iota(jnp.int32, (span, LANES), 1)
    i = lax.broadcasted_iota(jnp.int32, (LANES, span), 0)
    m = lax.broadcasted_iota(jnp.int32, (LANES, span), 1)
    down_ref[...] = jnp.zeros_like(down_ref)
    for s in range(scales):

        def one_tap(t, carry, s=s):
            down, across = carry
            tap = taps_ref[s, t]
            return jnp.where(k - n == t, tap, down), jnp.where(m - i == t, tap, across)

        down, across = lax.fori_loop(
            0,
            taps,
            one_tap,
            (jnp.zeros((span, LANES), jnp.float32), jnp.zeros((LANES, span), jnp.float32)),
            unroll=3,
        )
        across_ref[s] = across.astype(across_ref.dtype)
        down = down.astype(down_ref.dtype)
        for tile in range(COL_TILE // LANES):
            start = LANES - width + tile * LANES
            down_ref[s, start : start + span, tile * LANES : (tile + 1) * LANES] = down


def smooth_kernel(count, order_ref, taps_ref, x_ref, taper_in, out_ref, x_buf, taper_ref, across_ref, down_ref, y_ref, smooth_ref, acc_ref, stage_ref, local_sem, taper_sem, halo_send, halo_recv, send_sem, recv_sem):
    corr, scales, rows, side = x_ref.shape
    width = (taps_ref.shape[1] - 1) // 2
    tiles = side // COL_TILE
    me = lax.axis_index("strip")
    right, left = lax.rem(me + 1, count), lax.rem(me + count - 1, count)
    loads = [
        pltpu.make_async_copy(x_ref.at[c], x_buf.at[c, :, pl.ds(width, rows)], local_sem.at[c])
        for c in range(corr)
    ]
    taper_load = pltpu.make_async_copy(taper_in, taper_ref, taper_sem)
    for load in loads:
        load.start()
    taper_load.start()
    barrier = pltpu.get_barrier_semaphore()
    for off in range(1, count):
        pl.semaphore_signal(
            barrier, inc=1, device_id={"strip": lax.rem(me + off, count)}, device_id_type=MESH
        )
    pl.semaphore_wait(barrier, count - 1)
    halos = []
    for c in range(corr):
        pair = []
        for way, (start, landing, peer) in enumerate(
            ((rows - width, 0, right), (0, rows + width, left))
        ):
            pair.append(
                pltpu.make_async_remote_copy(
                    src_ref=x_ref.at[c, :, pl.ds(start, width)],
                    dst_ref=x_buf.at[c, :, pl.ds(landing, width)],
                    send_sem=halo_send.at[c, way],
                    recv_sem=halo_recv.at[c, way],
                    device_id={"strip": peer},
                    device_id_type=MESH,
                )
            )
        for copy in pair:
            copy.start()
        halos.append(pair)
    fill_bands(taps_ref, across_ref, down_ref, width)
    y_ref[:, :, 0:LANES] = jnp.zeros((scales, rows, LANES), y_ref.dtype)
    y_ref[:, :, LANES + side : 2 * LANES + side] = jnp.zeros((scales, rows, LANES), y_ref.dtype)
    sends = []
    for c in range(corr):
        loads[c].wait()
        for copy in halos[c]:
            copy.wait()

        @pl.when(me == 0)
        def _():
            x_buf[c, :, 0:width] = jnp.zeros((scales, width, side), x_buf.dtype)

        @pl.when(me == count - 1)
        def _():
            x_buf[c, :, rows + width : rows + 2 * width] = jnp.zeros((scales, width, side), x_buf.dtype)

        for s in range(scales):
            for b in range(rows // LANES):
                part = x_buf[c, s, b * LANES : (b + 1) * LANES + 2 * width]
                y = jnp.dot(across_ref[s], part, preferred_element_type=jnp.float32)
                y_ref[s, b * LANES : (b + 1) * LANES, LANES : LANES + side] = y.astype(y_ref.dtype)

        def one_tile(tile, carry):
            first = pl.multiple_of(tile * COL_TILE, COL_TILE)
            smoothed = jnp.zeros((rows, COL_TILE), jnp.float32)
            for s in range(scales):
                smoothed += jnp.dot(
                    y_ref[s, :, pl.ds(first, COL_TILE + 2 * LANES)],
                    down_ref[s],
                    preferred_element_type=jnp.float32,
                )
            smooth_ref[:, pl.ds(first, COL_TILE)] = smoothed.astype(smooth_ref.dtype)
            return carry

        lax.fori_loop(0, tiles, one_tile, 0, unroll=2)
        if c == 0:
            taper_load.wait()
        acc = jnp.dot(smooth_ref[...], taper_ref[...], preferred_element_type=jnp.float32)
        for d in range(count):
            acc_ref[d] = acc[:, d * LANES : (d + 1) * LANES]
        for d in range(count):
            stage_ref[c, d] = acc_ref[order_ref[d]].astype(stage_ref.dtype)
        for off in range(1, count):
            peer = lax.rem(me + off, count)
            copy = pltpu.make_async_remote_copy(
                src_ref=stage_ref.at[c, peer],
                dst_ref=out_ref.at[me, c],
                send_sem=send_sem.at[c, off],
                recv_sem=recv_sem.at[c, off],
                device_id={"strip": peer},
                device_id_type=MESH,
            )
            copy.start()
            sends.append(copy)
        out_ref[me, c] = stage_ref[c, me]
    for copy in sends:
        copy.wait()


def regrouped_products(comp, kernels, taper, order):
    corr, scales, rows, side = comp.shape
    taps = kernels.shape[1]
    count = lax.axis_size("strip")
    whole = pl.BlockSpec(memory_space=pltpu.VMEM)
    scalars = pl.BlockSpec(memory_space=pltpu.SMEM)
    remote = pl.BlockSpec(memory_space=pl.ANY)
    return pl.pallas_call(
        functools.partial(smooth_kernel, count),
        in_specs=[scalars, scalars, remote, remote],
        out_specs=whole,
        scratch_shapes=[
            pltpu.VMEM((corr, scales, rows + taps - 1, side), jnp.bfloat16),
            pltpu.VMEM(taper.shape, jnp.bfloat16),
            pltpu.VMEM((scales, LANES, LANES + taps - 1), jnp.bfloat16),
            pltpu.VMEM((scales, COL_TILE + 2 * LANES, COL_TILE), jnp.bfloat16),
            pltpu.VMEM((scales, rows, side + 2 * LANES), jnp.bfloat16),
            pltpu.VMEM((rows, side), jnp.bfloat16),
            pltpu.VMEM((count, rows, LANES), jnp.float32),
            pltpu.VMEM((corr, count, rows, LANES), jnp.bfloat16),
            pltpu.SemaphoreType.DMA((corr,)),
            pltpu.SemaphoreType.DMA,
            pltpu.SemaphoreType.DMA((corr, 2)),
            pltpu.SemaphoreType.DMA((corr, 2)),
            pltpu.SemaphoreType.DMA((corr, count)),
            pltpu.SemaphoreType.DMA((corr, count)),
        ],
        out_shape=jax.ShapeDtypeStruct((count, corr, rows, LANES), jnp.bfloat16),
        compiler_params=pltpu.CompilerParams(
            collective_id=0, has_side_effects=True, vmem_limit_bytes=60 * 1024 * 1024
        ),
        name="regrouped_products",
    )(order, kernels, comp, taper)


def exchange_kernel(count, order_ref, finished_ref, out_ref, stage_ref, send_sem, recv_sem):
    corr = finished_ref.shape[0]
    me = lax.axis_index("facet")
    barrier = pltpu.get_barrier_semaphore()
    for off in range(1, count):
        pl.semaphore_signal(
            barrier, inc=1, device_id={"facet": lax.rem(me + off, count)}, device_id_type=MESH
        )
    for d in range(count):
        for c in range(corr):
            stage_ref[d, c] = finished_ref[c, order_ref[d]]
    pl.semaphore_wait(barrier, count - 1)
    copies = []
    for off in range(1, count):
        peer = lax.rem(me + off, count)
        copy = pltpu.make_async_remote_copy(
            src_ref=stage_ref.at[peer],
            dst_ref=out_ref.at[me],
            send_sem=send_sem.at[off],
            recv_sem=recv_sem.at[off],
            device_id={"facet": peer},
            device_id_type=MESH,
        )
        copy.start()
        copies.append(copy)
    out_ref[me] = stage_ref[me]
    for copy in copies:
        copy.wait()


def exchanged(finished, order):
    corr, count, rows, cols = finished.shape
    whole = pl.BlockSpec(memory_space=pltpu.VMEM)
    shape = (count, corr, rows, cols)
    return pl.pallas_call(
        functools.partial(exchange_kernel, count),
        in_specs=[pl.BlockSpec(memory_space=pltpu.SMEM), whole],
        out_specs=whole,
        scratch_shapes=[
            pltpu.VMEM(shape, finished.dtype),
            pltpu.SemaphoreType.DMA((count,)),
            pltpu.SemaphoreType.DMA((count,)),
        ],
        out_shape=jax.ShapeDtypeStruct(shape, finished.dtype),
        compiler_params=pltpu.CompilerParams(collective_id=1, has_side_effects=True),
        name="exchanged",
    )(order, finished)


def looked_up(row, index):
    low, high = index % LANES, index // LANES
    out = None
    for chunk in range(row.shape[1] // LANES):
        table = jnp.broadcast_to(row[:, chunk * LANES : (chunk + 1) * LANES], index.shape)
        got = jnp.take_along_axis(table, low, axis=1, mode="promise_in_bounds")
        out = got if out is None else jnp.where(high == chunk, got, out)
    return out


def gain_kernel(gains_ref, index_ref, out_ref):
    p, q = index_ref[:, 0, :], index_ref[:, 1, :]
    for c in range(gains_ref.shape[0]):
        row = gains_ref[c : c + 1, :]
        out_ref[:, c, :] = looked_up(row, p) * looked_up(row, q)


def gain_products(gains, index):
    rows = index.shape[0]
    step = min(rows, 128)
    return pl.pallas_call(
        gain_kernel,
        grid=(rows // step,),
        in_specs=[
            pl.BlockSpec(gains.shape, lambda j: (0, 0)),
            pl.BlockSpec((step,) + index.shape[1:], lambda j: (j, 0, 0)),
        ],
        out_specs=pl.BlockSpec((step, gains.shape[0], index.shape[2]), lambda j: (j, 0, 0)),
        out_shape=jax.ShapeDtypeStruct((rows, gains.shape[0], index.shape[2]), jnp.float32),
        name="gain_products",
    )(gains, index)


ALIGN = 16


def degrid_kernel(corner_ref, target_ref, mine_ref, cols_ref, rows_ref, offset_ref, subgrid_ref, out_ref, turned_ref):
    facets, corr = mine_ref.shape[0], mine_ref.shape[1]
    side = cols_ref.shape[1]
    blocks, vis = offset_ref.shape[0], offset_ref.shape[2]
    tall, wide = TILE + ALIGN, 2 * LANES
    row_mats = jnp.concatenate([rows_ref[f] for f in range(facets)], axis=1)
    across = (((1,), (1,)), ((), ()))
    for c in range(corr):
        spread = jnp.concatenate(
            [
                lax.dot_general(
                    cols_ref[f], mine_ref[f, c], across, preferred_element_type=jnp.float32
                ).astype(jnp.bfloat16)
                for f in range(facets)
            ],
            axis=1,
        )
        subgrid_ref[c] = lax.dot_general(
            row_mats, spread, across, preferred_element_type=jnp.float32
        ).astype(jnp.bfloat16)
        turned_ref[c] = lax.dot_general(
            spread, row_mats, across, preferred_element_type=jnp.float32
        ).astype(jnp.bfloat16)
    out_ref[...] = jnp.zeros_like(out_ref)
    row_places = lax.broadcasted_iota(jnp.int32, (wide, vis), 0)
    col_places = lax.broadcasted_iota(jnp.int32, (tall, vis), 0)
    factor = -0.5 / (KERNEL_WIDTH * KERNEL_WIDTH)

    def weights(places, offset):
        delta = places.astype(jnp.float32) - offset
        inside = (places >= 0) & (places < TILE)
        return jnp.where(inside, jnp.exp(factor * (delta * delta)), 0.0)

    def one_block(k, carry):
        r, q = corner_ref[k, 0], corner_ref[k, 1]
        r0 = pl.multiple_of(jnp.minimum(r // LANES * LANES, side - wide), LANES)
        q0 = pl.multiple_of(jnp.minimum(q // ALIGN * ALIGN, side - tall), ALIGN)
        offsets = offset_ref[k]
        row_weights = weights(row_places - (r - r0), offsets[0:1]).astype(jnp.bfloat16)
        col_weights = weights(col_places - (q - q0), offsets[1:2])
        tile = jnp.concatenate(
            [turned_ref[c, pl.ds(q0, tall), pl.ds(r0, wide)] for c in range(corr)], axis=0
        )
        along = jnp.dot(tile, row_weights, preferred_element_type=jnp.float32)
        values = [
            jnp.sum(along[c * tall : (c + 1) * tall] * col_weights, axis=0, keepdims=True)
            for c in range(corr)
        ]
        out_ref[target_ref[k]] = jnp.concatenate(values, axis=0).astype(out_ref.dtype)
        return carry

    lax.fori_loop(0, blocks, one_block, 0, unroll=4)


def formed_and_predicted(mine, finish_cols, finish_rows, corners, offsets, target, slots):
    corr = mine.shape[1]
    side = finish_cols.shape[1]
    vis = offsets.shape[2]
    whole = pl.BlockSpec(memory_space=pltpu.VMEM)
    scalars = pl.BlockSpec(memory_space=pltpu.SMEM)
    return pl.pallas_call(
        degrid_kernel,
        in_specs=[scalars, scalars, whole, whole, whole, whole],
        out_specs=[whole, whole],
        out_shape=[
            jax.ShapeDtypeStruct((corr, side, side), jnp.bfloat16),
            jax.ShapeDtypeStruct((slots, corr, vis), jnp.bfloat16),
        ],
        scratch_shapes=[pltpu.VMEM((corr, side, side), jnp.bfloat16)],
        compiler_params=pltpu.CompilerParams(vmem_limit_bytes=32 * 1024 * 1024),
        name="formed_and_predicted",
    )(corners, target, mine, finish_cols, finish_rows, offsets)


def inverse_of(perm):
    count = perm.shape[0]
    places = jnp.arange(count, dtype=jnp.int32)
    return jnp.sum(jnp.where(perm[None, :] == places[:, None], places[None, :], 0), axis=1)


def on_device(
    sky_components,
    scale_kernels,
    row_taper,
    col_taper,
    finish_rows,
    finish_cols,
    subgrid_owner,
    block_cell,
    vis_offset,
    block_owner,
    observed,
    antenna_pair_index,
    gains,
):
    n_facet = lax.axis_size("facet")
    n_strip = lax.axis_size("strip")
    devices = n_facet * n_strip
    comp = sky_components[0]
    corr = comp.shape[0]
    rows = comp.shape[2]
    facet_side = comp.shape[3]
    contrib_side = finish_cols.shape[2]
    sub_rows = row_taper.shape[2] // contrib_side
    sub_cols = col_taper.shape[2] // contrib_side
    col_perm = subgrid_owner[:sub_cols] % n_strip
    row_perm = subgrid_owner.reshape(sub_rows, sub_cols)[:, 0] // n_strip
    col_inverse = inverse_of(col_perm)
    row_inverse = inverse_of(row_perm)
    regrouped = regrouped_products(comp, scale_kernels, col_taper[0], col_inverse)
    all_rows = row_taper[0].reshape(n_strip, rows, sub_rows * contrib_side)
    finished = jnp.einsum(
        "xrm,xcrj->cmj", all_rows, regrouped, preferred_element_type=jnp.float32
    ).astype(jnp.bfloat16)
    mine = exchanged(finished.reshape(corr, sub_rows, contrib_side, contrib_side), row_inverse)
    blocks = block_owner.shape[0]
    visibility_block = observed.shape[2]
    dest = block_owner[:, 0]
    same = dest[:, None] == dest[None, :]
    order = jnp.arange(blocks, dtype=jnp.int32)
    earlier = order[None, :] < order[:, None]
    rank = jnp.sum((same & earlier).astype(jnp.int32), axis=1)
    capacity = observed.shape[0] // devices
    target = dest * capacity + rank
    subgrid, outgoing_vis = formed_and_predicted(
        mine, finish_cols, finish_rows, block_cell, vis_offset, target, devices * capacity
    )
    outgoing_vis = outgoing_vis.reshape(devices, capacity, corr, visibility_block)
    arrived = lax.all_to_all(
        outgoing_vis, ("facet", "strip"), split_axis=0, concat_axis=0, tiled=True
    ).astype(jnp.float32)
    placed = arrived.reshape(devices * capacity, corr, visibility_block)
    product = gain_products(gains, antenna_pair_index)
    residual = observed - product * placed
    return (subgrid[None], residual)


def solution(mesh):
    placed = (
        P("facet", None, None, "strip", None),
        P(),
        P("facet", None, None),
        P("facet", None, None),
        P(),
        P(),
        P(),
        P(("facet", "strip"), None),
        P(("facet", "strip"), None, None),
        P(("facet", "strip"), None),
        P(("facet", "strip"), None, None),
        P(("facet", "strip"), None, None),
        P(),
    )
    return jax.shard_map(
        on_device,
        mesh=mesh,
        in_specs=placed,
        out_specs=(P(("facet", "strip"), None, None, None), P(("facet", "strip"), None, None)),
        check_vma=False,
    )
```

profile of v0, /device:TPU:0, one launch (start us, length us, event | category | flops | bytes accessed | tf_op | source)
XLA Modules:
  0.0 74.6 jit_solution(16543966142662122508)
XLA Ops:
  0.6 0.0 copy-start
  0.6 0.8 %and_select_fusion = s32[8]{0:T(128)S(1)} fusion(s32[32]{0:T(128)} %param.19), kind=kLoop, calls=%fused_computation.15 | loop fusion | flops 88 | bytes 64 | tf_op jit(solution)/shard_map/jit(remainder)/select_n | solution.py:374
  1.5 0.7 reshape.49
  2.2 0.6 select_reduce_fusion.order_ref
  2.8 31.3 %regrouped_products.1 = bf16[8,2,256,128]{3,2,1,0:T(8,128)(2,1)} custom-call(s32[8]{0:T(128)} %select_reduce_fusion.order_ref, f32[4,33]{1,0:T(4,128)} %taps_ref.1, bf16[2,4,256,2048]{3,2,1,0:T(8,128)(2,1)} %bitcast.26, bf16[2048,1024]{1,0:T(8,128)(2,1)} %bitcast.27), custom_call_target="tpu_custom_call" | custom-call | tf_op jit(solution)/shard_map/regrouped_products/pallas_call | solution.py:156
  34.1 0.0 copy-done
  34.2 0.0 copy-start.6
  34.2 0.0 copy-start.7
  34.2 0.0 copy-start.2
  34.2 0.0 copy-start.3
  34.2 0.0 copy-start.4
  34.2 2.0 %fusion.1 = bf16[2,512,128]{1,2,0:T(8,128)(2,1)S(1)} fusion(bf16[8,2,256,128]{3,2,1,0:T(8,128)(2,1)} %regrouped_products.1, bf16[8,256,512,1]{2,1,3,0:T(8,128)(2,1)S(1)} %bitcast.25), kind=kOutput, calls=%fused_computation.2 | convolution fusion | flops 537001984 | bytes 3407872 | tf_op jit(solution)/shard_map/xrm,xcrj->cmj/dot_general | solution.py:380
  36.3 0.8 %copy.22 = bf16[2,512,128]{2,1,0:T(8,128)(2,1)} copy(bf16[2,512,128]{1,2,0:T(8,128)(2,1)S(1)} %fusion.1) | data formatting | bytes 524288 | tf_op jit(solution)/shard_map/convert_element_type | solution.py:382
  37.1 0.0 copy-start.5
  37.1 0.1 slice_reduce_fusion
  37.2 0.6 select_reduce_fusion.1.order_ref
  37.9 0.0 copy-done.6
  37.9 0.1 copy.23.corner_ref
  38.0 0.0 copy-done.7
  38.0 0.2 convert_reduce_fusion
  38.1 11.5 %exchanged.1.mine_ref = bf16[4,2,128,128]{3,2,1,0:T(8,128)(2,1)} custom-call(s32[4]{0:T(128)} %select_reduce_fusion.1.order_ref, bf16[2,4,128,128]{3,2,1,0:T(8,128)(2,1)} %bitcast.28), custom_call_target="tpu_custom_call" | custom-call | tf_op jit(solution)/shard_map/exchanged/pallas_call | solution.py:218
  49.7 0.0 copy-done.2
  49.7 0.0 copy-done.3
  49.7 0.0 copy-done.4
  49.7 0.0 copy-start.1
  49.7 0.9 %copy-done.1 = bf16[4,2,128,128]{3,2,1,0:T(8,128)(2,1)S(1)} copy-done((bf16[4,2,128,128]{3,2,1,0:T(8,128)(2,1)S(1)}, bf16[4,2,128,128]{3,2,1,0:T(8,128)(2,1)}, u32[]{:S(2)}) %copy-start.1) | copy-done | bytes 262168
  50.7 9.5 %formed_and_predicted.1 = (bf16[2,512,512]{2,1,0:T(8,128)(2,1)}, bf16[128,2,128]{2,1,0:T(2,128)(2,1)}) custom-call(s32[64,2]{1,0:T(8,128)S(1)} %copy.23.corner_ref, s32[64]{0:T(128)S(1)} %multiply_add_fusion.target_ref, bf16[4,2,128,128]{3,2,1,0:T(8,128)(2,1)S(1)} %copy-done.1, bf16[4,512,128]{2,1,0:T(8,128)(2,1)S(1)} %copy-done.2, ...), custom_call_target="tpu_custom_call" | custom-call | tf_op jit(solution)/shard_map/formed_and_predicted/pallas_call | solution.py:329
  60.2 5.3 %all-to-all-start = ((bf16[32,4,2,128]{3,2,1,0:T(2,128)(2,1)}), bf16[32,4,2,128]{3,2,1,0:T(2,128)(2,1)S(1)}, u32[]{:S(2)}, u32[]{:S(2)}) async-start(bf16[32,4,2,128]{3,2,1,0:T(2,128)(2,1)} %bitcast.10), calls=%async_computation | async-start | bytes 131072 | tf_op jit(solution)/shard_map/all_to_all | solution.py:397
  65.5 3.3 %gain_products.1 = f32[128,2,128]{2,1,0:T(2,128)} custom-call(f32[2,512]{1,0:T(2,128)} %gains_ref.1, s32[128,2,128]{2,1,0:T(2,128)} %index_ref.1), custom_call_target="tpu_custom_call" | custom-call | tf_op jit(solution)/shard_map/gain_products/pallas_call | solution.py:253
  68.8 4.1 %all-to-all-done = bf16[32,4,2,128]{3,2,1,0:T(2,128)(2,1)S(1)} async-done(((bf16[32,4,2,128]{3,2,1,0:T(2,128)(2,1)}), bf16[32,4,2,128]{3,2,1,0:T(2,128)(2,1)S(1)}, u32[]{:S(2)}, u32[]{:S(2)}) %all-to-all-start) | async-done | bytes 65568 | tf_op jit(solution)/shard_map/all_to_all | solution.py:397
  72.9 0.0 copy-done.5
  72.9 1.7 %fusion.2 = f32[128,2,128]{2,1,0:T(2,128)} fusion(f32[128,2,128]{2,1,0:T(2,128)S(1)} %copy-done.5, f32[128,2,128]{2,1,0:T(2,128)} %gain_products.1, bf16[32,4,2,128]{3,2,1,0:T(2,128)(2,1)S(1)} %all-to-all-done), kind=kLoop, calls=%fused_computation.4 | loop fusion | flops 98304 | bytes 458752 | tf_op jit(solution)/shard_map/sub | solution.py:402
  (2 shorter events, 0.0 us)
Async XLA Ops:
  0.6 33.5 %copy-start = (bf16[1,2048,512]{2,1,0:T(8,128)(2,1)S(1)}, bf16[1,2048,512]{2,1,0:T(8,128)(2,1)}, u32[]{:S(2)}) copy-start(bf16[1,2048,512]{2,1,0:T(8,128)(2,1)} %param.15) | copy-start | bytes 6291460
  34.2 3.7 %copy-start.6 = (s32[64,2]{0,1:T(2,128)S(1)}, s32[64,2]{0,1:T(2,128)}, u32[]{:S(2)}) copy-start(s32[64,2]{0,1:T(2,128)} %param.20) | copy-start | bytes 1540
  34.2 3.8 %copy-start.7 = (s32[64,1]{0,1:T(1,128)S(1)}, s32[64,1]{0,1:T(1,128)}, u32[]{:S(2)}) copy-start(s32[64,1]{0,1:T(1,128)} %param.22) | copy-start | bytes 772
  34.2 15.5 %copy-start.2 = (bf16[4,512,128]{2,1,0:T(8,128)(2,1)S(1)}, bf16[4,512,128]{2,1,0:T(8,128)(2,1)}, u32[]{:S(2)}) copy-start(bf16[4,512,128]{2,1,0:T(8,128)(2,1)} %cols_ref.1) | copy-start | bytes 1572868
  34.2 15.5 %copy-start.3 = (bf16[4,512,128]{2,1,0:T(8,128)(2,1)S(1)}, bf16[4,512,128]{2,1,0:T(8,128)(2,1)}, u32[]{:S(2)}) copy-start(bf16[4,512,128]{2,1,0:T(8,128)(2,1)} %rows_ref.1) | copy-start | bytes 1572868
  34.2 15.5 %copy-start.4 = (f32[64,2,128]{2,1,0:T(2,128)S(1)}, f32[64,2,128]{2,1,0:T(2,128)}, u32[]{:S(2)}) copy-start(f32[64,2,128]{2,1,0:T(2,128)} %offset_ref.1) | copy-start | bytes 196612
  37.1 35.8 %copy-start.5 = (f32[128,2,128]{2,1,0:T(2,128)S(1)}, f32[128,2,128]{2,1,0:T(2,128)}, u32[]{:S(2)}) copy-start(f32[128,2,128]{2,1,0:T(2,128)} %param.23) | copy-start | bytes 393220
  49.7 1.0 %copy-start.1 = (bf16[4,2,128,128]{3,2,1,0:T(8,128)(2,1)S(1)}, bf16[4,2,128,128]{3,2,1,0:T(8,128)(2,1)}, u32[]{:S(2)}) copy-start(bf16[4,2,128,128]{3,2,1,0:T(8,128)(2,1)} %exchanged.1.mine_ref) | copy-start | bytes 786436
  60.2 12.8 %all-to-all-start = ((bf16[32,4,2,128]{3,2,1,0:T(2,128)(2,1)}), bf16[32,4,2,128]{3,2,1,0:T(2,128)(2,1)S(1)}, u32[]{:S(2)}, u32[]{:S(2)}) async-start(bf16[32,4,2,128]{3,2,1,0:T(2,128)(2,1)} %bitcast.10), calls=%async_computation | async-start | bytes 131072 | tf_op jit(solution)/shard_map/all_to_all | solution.py:397
where the time goes:
time: 74.9 us; the launch traced here: 74.6 us
  Pallas kernels  55.6 us (74%)
  starting transfers between devices  5.34 us (7%)
  waiting for transfers between devices  4.15 us (6%)
  other arithmetic  3.92 us (5%)
  local copies, waits for them, and re-layouts  2.77 us (4%)
  matrix products  2.03 us (3%)
  between operations  0.76 us (1%)
    pallas_call x1, Pallas kernels, regrouped_products(): pl.pallas_call(functools.partial(smooth_kernel, count), in_specs=[scalars...  31.3 us
    pallas_call x1, Pallas kernels, exchanged(): pl.pallas_call(functools.partial(exchange_kernel, count), in_specs=[pl.Bl...  11.5 us
    pallas_call x1, Pallas kernels, formed_and_predicted(): pl.pallas_call(degrid_kernel, in_specs=[scalars, scalars, whole, whole, w...  9.5 us
    all_to_all x1, starting transfers between devices, on_device(): lax.all_to_all(outgoing_vis, ('facet', 'strip'), split_axis=0, concat_axi...  5.34 us
    all_to_all x1, waiting for transfers between devices, on_device(): lax.all_to_all(outgoing_vis, ('facet', 'strip'), split_axis=0, concat_axi...  4.15 us
    pallas_call x1, Pallas kernels, gain_products(): pl.pallas_call(gain_kernel, grid=(rows // step,), in_specs=[pl.BlockSpec(...  3.26 us
    dot_general x1, matrix products, on_device(): jnp.einsum('xrm,xcrj->cmj', all_rows, regrouped, preferred_element_type=j...  2.03 us
    sub x1, other arithmetic, on_device(): residual = observed - product * placed  1.66 us
  transfers between devices with their start and end apart: 1, of which 1 were waited for; matrix products, arithmetic and copies ran while one was open for 0% of the time, Pallas kernels for 4%

commit v1 on v0

v1 whole, which is shorter than its diff:
```python
import functools

import jax
import jax.numpy as jnp
from jax import lax
from jax.experimental import pallas as pl
from jax.experimental.pallas import tpu as pltpu
from jax.sharding import PartitionSpec as P

TILE = 32
KERNEL_WIDTH = 1.5
LANES = 128
COL_TILE = 256
ALIGN = 16
TALL = TILE + ALIGN
WIDE = LANES + TILE
MESH = pl.DeviceIdType.MESH
ACROSS = (((1,), (1,)), ((), ()))


def mm(a, b):
    return jnp.dot(a, b, preferred_element_type=jnp.float32)


def fill_bands(taps_ref, pad_ref, across_ref, down_ref, width):
    scales, taps = taps_ref.shape
    span = LANES + taps - 1
    pad_ref[...] = jnp.zeros_like(pad_ref)
    pad_ref[:, 0:taps] = taps_ref[...]
    down_ref[...] = jnp.zeros_like(down_ref)
    for s in range(scales):
        row = jnp.broadcast_to(pad_ref[s : s + 1, :], (LANES, 2 * LANES))
        band = pltpu.roll(row, 0, 1, stride=1, stride_axis=0)
        across_ref[s] = band[:, :span].astype(across_ref.dtype)
        down = band.T[:span].astype(down_ref.dtype)
        for tile in range(COL_TILE // LANES):
            start = LANES - width + tile * LANES
            down_ref[s, start : start + span, tile * LANES : (tile + 1) * LANES] = down


def position_of(values, wanted):
    place = 0
    for j, value in enumerate(values):
        gap = value - wanted
        place += j * jnp.maximum(1 - gap * gap, 0)
    return jnp.minimum(place, len(values) - 1)


def looked_up(row, index):
    low, high = index % LANES, index // LANES
    out = None
    for chunk in range(row.shape[1] // LANES):
        table = jnp.broadcast_to(row[:, chunk * LANES : (chunk + 1) * LANES], index.shape)
        got = jnp.take_along_axis(table, low, axis=1, mode="promise_in_bounds")
        out = got if out is None else jnp.where(high == chunk, got, out)
    return out


def whole_kernel(
    n_facet,
    n_strip,
    owner_ref,
    corner_ref,
    taps_ref,
    dest_ref,
    gains_ref,
    x_ref,
    col_in,
    row_in,
    frows_in,
    fcols_in,
    offset_in,
    index_in,
    observed_in,
    subgrid_out,
    residual_out,
    x_buf,
    col_taper,
    row_taper,
    frows,
    fcols,
    offsets,
    index,
    observed,
    pad_ref,
    across_ref,
    down_ref,
    y_ref,
    smooth_ref,
    stage,
    grouped,
    stage2,
    mine,
    row_mats,
    spread,
    turned,
    subgrid,
    row_weights,
    col_weights,
    onehot,
    values,
    outgoing,
    arrived,
    wide,
    product,
    load_sem,
    halo_send,
    halo_recv,
    strip_send,
    strip_recv,
    facet_send,
    facet_recv,
    vis_send,
    vis_recv,
    out_sem,
    ready_sem,
):
    corr, scales, rows, side = x_ref.shape
    width = (taps_ref.shape[1] - 1) // 2
    tiles = side // COL_TILE
    contrib = fcols.shape[2]
    sub_side = fcols.shape[1]
    blocks = offsets.shape[0]
    vis = offsets.shape[2]
    devices = n_facet * n_strip
    capacity = observed.shape[0] // devices
    sub_cols = col_taper.shape[0]
    sub_rows = row_taper.shape[0]
    f_me = lax.axis_index("facet")
    s_me = lax.axis_index("strip")
    me = f_me * n_strip + s_me

    x_loads = [
        pltpu.make_async_copy(x_ref.at[c], x_buf.at[c, :, pl.ds(width, rows)], load_sem.at[c])
        for c in range(corr)
    ]
    others = [
        pltpu.make_async_copy(src, dst, load_sem.at[corr + n])
        for n, (src, dst) in enumerate(
            (
                (index_in, index),
                (offset_in, offsets),
                (frows_in, frows),
                (fcols_in, fcols),
                (observed_in, observed),
            )
        )
    ]
    index_load, offset_load, frows_load, fcols_load, observed_load = others
    col_loads = [
        pltpu.make_async_copy(
            col_in.at[:, pl.ds(b * contrib, contrib)], col_taper.at[b], load_sem.at[corr + 5 + b]
        )
        for b in range(sub_cols)
    ]
    row_loads = [
        pltpu.make_async_copy(
            row_in.at[:, pl.ds(a * contrib, contrib)],
            row_taper.at[a],
            load_sem.at[corr + 5 + sub_cols + a],
        )
        for a in range(sub_rows)
    ]
    for load in x_loads + col_loads + others + row_loads:
        load.start()

    barrier = pltpu.get_barrier_semaphore()
    for off in range(1, n_strip):
        pl.semaphore_signal(
            barrier, inc=1, device_id={"strip": lax.rem(s_me + off, n_strip)}, device_id_type=MESH
        )
    for off in range(1, n_facet):
        pl.semaphore_signal(
            barrier, inc=1, device_id={"facet": lax.rem(f_me + off, n_facet)}, device_id_type=MESH
        )
    fill_bands(taps_ref, pad_ref, across_ref, down_ref, width)
    y_ref[:, :, 0:LANES] = jnp.zeros((scales, rows, LANES), y_ref.dtype)
    y_ref[:, :, LANES + side : 2 * LANES + side] = jnp.zeros((scales, rows, LANES), y_ref.dtype)
    pl.semaphore_wait(barrier, n_strip + n_facet - 2)
    right, left = lax.rem(s_me + 1, n_strip), lax.rem(s_me + n_strip - 1, n_strip)
    halos = []
    for c in range(corr):
        pair = []
        for way, (start, landing, peer) in enumerate(
            ((rows - width, 0, right), (0, rows + width, left))
        ):
            copy = pltpu.make_async_remote_copy(
                src_ref=x_ref.at[c, :, pl.ds(start, width)],
                dst_ref=x_buf.at[c, :, pl.ds(landing, width)],
                send_sem=halo_send.at[c, way],
                recv_sem=halo_recv.at[c, way],
                device_id={"strip": peer},
                device_id_type=MESH,
            )
            copy.start()
            pair.append(copy)
        halos.append(pair)
    for off in range(1, n_strip):
        pl.semaphore_signal(
            ready_sem, inc=1, device_id={"strip": lax.rem(s_me + off, n_strip)}, device_id_type=MESH
        )
    col_perm = [lax.rem(owner_ref[b], n_strip) for b in range(sub_cols)]
    row_perm = [lax.div(owner_ref[a * sub_cols], n_strip) for a in range(sub_rows)]

    strip_copies = []
    for c in range(corr):
        x_loads[c].wait()
        for copy in halos[c]:
            copy.wait()

        @pl.when(s_me == 0)
        def _():
            x_buf[c, :, 0:width] = jnp.zeros((scales, width, side), x_buf.dtype)

        @pl.when(s_me == n_strip - 1)
        def _():
            x_buf[c, :, rows + width : rows + 2 * width] = jnp.zeros((scales, width, side), x_buf.dtype)

        for s in range(scales):
            for b in range(rows // LANES):
                part = x_buf[c, s, b * LANES : (b + 1) * LANES + 2 * width]
                y_ref[s, b * LANES : (b + 1) * LANES, LANES : LANES + side] = mm(
                    across_ref[s], part
                ).astype(y_ref.dtype)

        def one_tile(tile, carry):
            first = pl.multiple_of(tile * COL_TILE, COL_TILE)
            smoothed = jnp.zeros((rows, COL_TILE), jnp.float32)
            for s in range(scales):
                smoothed += mm(y_ref[s, :, pl.ds(first, COL_TILE + 2 * LANES)], down_ref[s])
            smooth_ref[:, pl.ds(first, COL_TILE)] = smoothed.astype(smooth_ref.dtype)
            return carry

        lax.fori_loop(0, tiles, one_tile, 0, unroll=2)
        if c == 0:
            for load in col_loads:
                load.wait()
        for off in range(1, n_strip + 1):
            peer = lax.rem(s_me + off, n_strip)
            b = position_of(col_perm, peer)
            got = mm(smooth_ref[...], col_taper[b]).astype(stage.dtype)
            if off == n_strip:
                grouped[s_me, c] = got
                continue
            stage[c, off] = got
            copy = pltpu.make_async_remote_copy(
                src_ref=stage.at[c, off],
                dst_ref=grouped.at[s_me, c],
                send_sem=strip_send.at[c, off],
                recv_sem=strip_recv.at[c, off],
                device_id={"strip": peer},
                device_id_type=MESH,
            )
            copy.start()
            strip_copies.append(copy)

    index_load.wait()
    for c in range(corr):
        row = gains_ref[c : c + 1, :]
        product[c] = looked_up(row, index[:, 0, :]) * looked_up(row, index[:, 1, :])
    dest = dest_ref[...]
    k_row = lax.broadcasted_iota(jnp.int32, (blocks, blocks), 0)
    k_col = lax.broadcasted_iota(jnp.int32, (blocks, blocks), 1)
    dest_wide = jnp.broadcast_to(dest, (blocks, blocks))
    dest_tall = jnp.sum(jnp.where(k_row == k_col, dest_wide, 0), axis=1, keepdims=True)
    same = (dest_tall == dest_wide) & (k_row < k_col)
    rank = jnp.sum(jnp.where(same, 1, 0), axis=0, keepdims=True)
    target = dest * capacity + rank
    code = jnp.concatenate([target * corr + c for c in range(corr)], axis=1)
    places = lax.broadcasted_iota(jnp.int32, onehot.shape, 0)
    onehot[...] = jnp.where(places == code, 1.0, 0.0).astype(onehot.dtype)
    r_blocks, q_blocks = sub_side // LANES, sub_side // ALIGN
    turned[:, r_blocks] = jnp.zeros((corr,) + turned.shape[2:], turned.dtype)
    turned[:, :, q_blocks] = jnp.zeros((corr, r_blocks + 1, ALIGN, LANES), turned.dtype)
    offset_load.wait()
    row_places = lax.broadcasted_iota(jnp.int32, (WIDE, vis), 0)
    col_places = lax.broadcasted_iota(jnp.int32, (TALL, vis), 0)
    factor = -0.5 / (KERNEL_WIDTH * KERNEL_WIDTH)

    def weights(spots, offset):
        delta = spots.astype(jnp.float32) - offset
        inside = (spots >= 0) & (spots < TILE)
        return jnp.where(inside, jnp.exp(factor * (delta * delta)), 0.0)

    def corner(k):
        r, q = corner_ref[0, k], corner_ref[1, k]
        rb = jnp.clip(lax.div(r, LANES), 0, r_blocks - 1)
        qb = jnp.clip(lax.div(q, ALIGN), 0, q_blocks - 2)
        return r - rb * LANES, q - qb * ALIGN, rb, qb

    def one_weight(k, carry):
        r_in, q_in, _, _ = corner(k)
        here = offsets[k]
        row_weights[k] = weights(row_places - r_in, here[0:1]).astype(row_weights.dtype)
        col_weights[k] = weights(col_places - q_in, here[1:2])
        return carry

    lax.fori_loop(0, blocks, one_weight, 0, unroll=2)
    frows_load.wait()
    fcols_load.wait()
    row_mats[...] = jnp.concatenate([frows[f] for f in range(n_facet)], axis=1)
    for load in row_loads:
        load.wait()

    facet_copies = []
    for c in range(corr):
        for copy in strip_copies[c * (n_strip - 1) : (c + 1) * (n_strip - 1)]:
            copy.wait()
        flipped = jnp.concatenate([grouped[x, c].T for x in range(n_strip)], axis=1)
        for off in range(1, n_facet + 1):
            peer = lax.rem(f_me + off, n_facet)
            a = position_of(row_perm, peer)
            got = mm(flipped, row_taper[a]).astype(stage2.dtype)
            if off == n_facet:
                mine[f_me, c] = got
                continue
            stage2[c, off] = got
            copy = pltpu.make_async_remote_copy(
                src_ref=stage2.at[c, off],
                dst_ref=mine.at[f_me, c],
                send_sem=facet_send.at[c, off],
                recv_sem=facet_recv.at[c, off],
                device_id={"facet": peer},
                device_id_type=MESH,
            )
            copy.start()
            facet_copies.append(copy)

    for c in range(corr):
        for copy in facet_copies[c * (n_facet - 1) : (c + 1) * (n_facet - 1)]:
            copy.wait()
        for f in range(n_facet):
            spread[c, :, f * contrib : (f + 1) * contrib] = mm(fcols[f], mine[f, c]).astype(spread.dtype)
        for rb in range(r_blocks):
            turned[c, rb, 0:q_blocks] = (
                lax.dot_general(
                    spread[c],
                    row_mats[rb * LANES : (rb + 1) * LANES],
                    ACROSS,
                    preferred_element_type=jnp.float32,
                )
                .astype(turned.dtype)
                .reshape(q_blocks, ALIGN, LANES)
            )

        def one_block(k, carry, c=c):
            _, _, rb, qb = corner(k)
            tile = jnp.concatenate(
                [
                    jnp.concatenate([turned[c, rb + j, qb + i] for j in range(2)], axis=1)
                    for i in range(TALL // ALIGN)
                ],
                axis=0,
            )
            along = mm(tile[:, :WIDE], row_weights[k])
            values[pl.ds(c * blocks + k, 1), :] = jnp.sum(along * col_weights[k], axis=0, keepdims=True)
            return carry

        lax.fori_loop(0, blocks, one_block, 0, unroll=8)

    outgoing[...] = (
        mm(onehot[...], values[...].astype(jnp.bfloat16))
        .astype(outgoing.dtype)
        .reshape(outgoing.shape)
    )
    pl.semaphore_wait(ready_sem, n_strip - 1)

    def vis_copy(off):
        peer = lax.rem(me + off, devices)
        return pltpu.make_async_remote_copy(
            src_ref=outgoing.at[peer],
            dst_ref=arrived.at[me],
            send_sem=vis_send.at[off],
            recv_sem=vis_recv.at[off],
            device_id={"facet": peer // n_strip, "strip": peer % n_strip},
            device_id_type=MESH,
        )

    def send_one(off, carry):
        vis_copy(off).start()
        return carry

    lax.fori_loop(1, devices, send_one, 0)
    arrived[me] = outgoing[me]
    subgrid_copies = []
    for c in range(corr):
        subgrid[c] = lax.dot_general(
            row_mats[...], spread[c], ACROSS, preferred_element_type=jnp.float32
        ).astype(subgrid.dtype)
        copy = pltpu.make_async_copy(subgrid.at[c], subgrid_out.at[c], out_sem.at[c])
        copy.start()
        subgrid_copies.append(copy)
    observed_load.wait()

    def wait_one(off, carry):
        vis_copy(off).wait()
        return carry

    lax.fori_loop(1, devices, wait_one, 0)
    wide[...] = arrived[...].astype(jnp.float32).reshape(wide.shape)
    for c in range(corr):
        placed = wide[pl.ds(c, devices * capacity, stride=corr), :]
        residual_out[:, c, :] = observed[:, c, :] - product[c] * placed
    for copy in subgrid_copies:
        copy.wait()


def on_device(
    sky_components,
    scale_kernels,
    row_taper,
    col_taper,
    finish_rows,
    finish_cols,
    subgrid_owner,
    block_cell,
    vis_offset,
    block_owner,
    observed,
    antenna_pair_index,
    gains,
):
    n_facet = lax.axis_size("facet")
    n_strip = lax.axis_size("strip")
    devices = n_facet * n_strip
    comp = sky_components[0]
    corr, scales, rows, side = comp.shape
    taps = scale_kernels.shape[1]
    sub_side, contrib = finish_cols.shape[1], finish_cols.shape[2]
    blocks, _, vis = vis_offset.shape
    sub_rows, sub_cols = row_taper.shape[2] // contrib, col_taper.shape[2] // contrib
    slots = observed.shape[0]
    per_device = slots // devices * corr
    whole = pl.BlockSpec(memory_space=pltpu.VMEM)
    scalars = pl.BlockSpec(memory_space=pltpu.SMEM)
    remote = pl.BlockSpec(memory_space=pl.ANY)
    bf16, f32 = jnp.bfloat16, jnp.float32
    dma = pltpu.SemaphoreType.DMA
    subgrid, residual = pl.pallas_call(
        functools.partial(whole_kernel, n_facet, n_strip),
        in_specs=[scalars, scalars, whole, whole, whole] + [remote] * 8,
        out_specs=[remote, whole],
        out_shape=[
            jax.ShapeDtypeStruct((corr, sub_side, sub_side), bf16),
            jax.ShapeDtypeStruct(observed.shape, f32),
        ],
        scratch_shapes=[
            pltpu.VMEM((corr, scales, rows + taps - 1, side), bf16),
            pltpu.VMEM((sub_cols, side, contrib), bf16),
            pltpu.VMEM((sub_rows, side, contrib), bf16),
            pltpu.VMEM(finish_rows.shape, bf16),
            pltpu.VMEM(finish_cols.shape, bf16),
            pltpu.VMEM(vis_offset.shape, f32),
            pltpu.VMEM(antenna_pair_index.shape, jnp.int32),
            pltpu.VMEM(observed.shape, f32),
            pltpu.VMEM((scales, 2 * LANES), f32),
            pltpu.VMEM((scales, LANES, LANES + taps - 1), bf16),
            pltpu.VMEM((scales, COL_TILE + 2 * LANES, COL_TILE), bf16),
            pltpu.VMEM((scales, rows, side + 2 * LANES), bf16),
            pltpu.VMEM((rows, side), bf16),
            pltpu.VMEM((corr, n_strip, rows, contrib), bf16),
            pltpu.VMEM((n_strip, corr, rows, contrib), bf16),
            pltpu.VMEM((corr, n_facet, contrib, contrib), bf16),
            pltpu.VMEM((n_facet, corr, contrib, contrib), bf16),
            pltpu.VMEM((sub_side, n_facet * contrib), bf16),
            pltpu.VMEM((corr, sub_side, n_facet * contrib), bf16),
            pltpu.VMEM((corr, sub_side // LANES + 1, sub_side // ALIGN + 1, ALIGN, LANES), bf16),
            pltpu.VMEM((corr, sub_side, sub_side), bf16),
            pltpu.VMEM((blocks, WIDE, vis), bf16),
            pltpu.VMEM((blocks, TALL, vis), f32),
            pltpu.VMEM((devices * per_device, corr * blocks), bf16),
            pltpu.VMEM((corr * blocks, vis), f32),
            pltpu.VMEM((devices, per_device, vis), bf16),
            pltpu.VMEM((devices, per_device, vis), bf16),
            pltpu.VMEM((devices * per_device, vis), f32),
            pltpu.VMEM((corr, slots, vis), f32),
            dma((corr + 5 + sub_cols + sub_rows,)),
            dma((corr, 2)),
            dma((corr, 2)),
            dma((corr, n_strip)),
            dma((corr, n_strip)),
            dma((corr, n_facet)),
            dma((corr, n_facet)),
            dma((devices,)),
            dma((devices,)),
            dma((corr,)),
            pltpu.SemaphoreType.REGULAR,
        ],
        compiler_params=pltpu.CompilerParams(
            collective_id=0, has_side_effects=True, vmem_limit_bytes=60 * 1024 * 1024
        ),
        name="sky_to_residual",
    )(
        subgrid_owner,
        block_cell.T,
        scale_kernels,
        block_owner.reshape(1, blocks),
        gains,
        comp,
        col_taper[0],
        row_taper[0],
        finish_rows,
        finish_cols,
        vis_offset,
        antenna_pair_index,
        observed,
    )
    return subgrid[None], residual


def solution(mesh):
    placed = (
        P("facet", None, None, "strip", None),
        P(),
        P("facet", None, None),
        P("facet", None, None),
        P(),
        P(),
        P(),
        P(("facet", "strip"), None),
        P(("facet", "strip"), None, None),
        P(("facet", "strip"), None),
        P(("facet", "strip"), None, None),
        P(("facet", "strip"), None, None),
        P(),
    )
    return jax.shard_map(
        on_device,
        mesh=mesh,
        in_specs=placed,
        out_specs=(P(("facet", "strip"), None, None, None), P(("facet", "strip"), None, None)),
        check_vma=False,
    )
```

time: 74.9 us -> 59.7 us (0.80)
  starting transfers between devices: 5.34 us -> 0 us
  waiting for transfers between devices: 4.15 us -> 0 us
  other arithmetic: 3.92 us -> 0 us
  matrix products: 2.03 us -> 0 us
  local copies, waits for them, and re-layouts: 2.77 us -> 3.83 us
    all_to_all x1 -> x0, starting transfers between devices: 5.34 us -> none  [on_device(): lax.all_to_all(outgoing_vis, ('facet', 'strip'), split_axis=0, concat_axi...]
    all_to_all x1 -> x0, waiting for transfers between devices: 4.15 us -> none  [on_device(): lax.all_to_all(outgoing_vis, ('facet', 'strip'), split_axis=0, concat_axi...]
    unnamed x17 -> x2, local copies, waits for them, and re-layouts: 1.08 us -> 3.83 us
    dot_general x1 -> x0, matrix products: 2.03 us -> none  [on_device(): jnp.einsum('xrm,xcrj->cmj', all_rows, regrouped, preferred_element_type=j...]
    sub x1 -> x0, other arithmetic: 1.66 us -> none  [on_device(): residual = observed - product * placed]
    reduce_sum x3 -> x0, other arithmetic: 1.43 us -> none  [the longest x2 1.26 us: inverse_of(): jnp.sum(jnp.where(perm[None, :] == places[:, None], places[None, :], 0),...]
    convert_element_type x1 -> x0, local copies, waits for them, and re-layouts: 0.84 us -> none  [on_device(): finished = jnp.einsum('xrm,xcrj->cmj', all_rows, regrouped, preferred_ele...]
    select_n x2 -> x0, other arithmetic: 0.83 us -> none  [the longest x1 0.81 us: on_device(): col_perm = subgrid_owner[:sub_cols] % n_strip]
  transfers between devices with their start and end apart: 1 -> 0, of which waited for: 1 -> 0; matrix products, arithmetic and copies ran while one was open for 0% -> 0% of each run, Pallas kernels for 4% -> 0%
where the time goes in v1:
time: 59.7 us; the launch traced here: 59.5 us
  Pallas kernels  55 us (92%)
  local copies, waits for them, and re-layouts  3.83 us (6%)
  between operations  0.64 us (1%)
    pallas_call x1, Pallas kernels, on_device(): pl.pallas_call(functools.partial(whole_kernel, n_facet, n_strip), in_spec...  55 us
    unnamed x2, local copies, waits for them, and re-layouts  3.83 us

profile of v1, /device:TPU:0, one launch (start us, length us, event | category | flops | bytes accessed | tf_op | source)
XLA Modules:
  0.0 59.5 jit_solution(478695269483738092)
XLA Ops:
  0.6 55.0 %sky_to_residual.1 = (bf16[2,512,512]{2,1,0:T(8,128)(2,1)}, f32[128,2,128]{2,1,0:T(2,128)}) custom-call(s32[32]{0:T(128)} %owner_ref.1, s32[2,64]{1,0:T(2,128)} %bitcast.10, f32[4,33]{1,0:T(4,128)} %taps_ref.1, s32[1,64]{1,0:T(1,128)} %bitcast.11, f32[2,512]{1,0:T(2,128)} %gains_ref.1, bf16[2,4,256,2048]{3,2,1,0:T(8,128)(2,1)} %bitcast.6, ...), custom_call_target="tpu_custom_call" | custom-call | tf_op jit(solution)/shard_map/sky_to_residual/pallas_call | solution.py:439
  55.7 2.3 %copy.17 = bf16[1,2,512,512]{3,2,1,0:T(8,128)(2,1)} copy(bf16[1,2,512,512]{3,2,1,0:T(8,128)(2,1)} %bitcast.9) | data formatting | bytes 2097152
  57.9 1.6 %copy.18 = f32[128,2,128]{2,1,0:T(2,128)} copy(f32[128,2,128]{2,1,0:T(2,128)} %get-tuple-element.9) | data formatting | bytes 262144

commit v2 on v1

--- a/solution.py
+++ b/solution.py
@@ -24,6 +24,7 @@
 
 def fill_bands(taps_ref, pad_ref, across_ref, down_ref, width):
     scales, taps = taps_ref.shape
+    tall, rows = across_ref.shape[1:]
     span = LANES + taps - 1
     pad_ref[...] = jnp.zeros_like(pad_ref)
     pad_ref[:, 0:taps] = taps_ref[...]
@@ -31,11 +32,26 @@
     for s in range(scales):
         row = jnp.broadcast_to(pad_ref[s : s + 1, :], (LANES, 2 * LANES))
         band = pltpu.roll(row, 0, 1, stride=1, stride_axis=0)
-        across_ref[s] = band[:, :span].astype(across_ref.dtype)
         down = band.T[:span].astype(down_ref.dtype)
         for tile in range(COL_TILE // LANES):
             start = LANES - width + tile * LANES
             down_ref[s, start : start + span, tile * LANES : (tile + 1) * LANES] = down
+        for first in range(0, tall, LANES):
+            size = min(LANES, tall - first)
+            line = jnp.broadcast_to(pad_ref[s : s + 1, 0:rows], (size, rows))
+            line = pltpu.roll(line, (rows + first - 2 * width) % rows, 1)
+            line = pltpu.roll(line, 0, 1, stride=1, stride_axis=0)
+            gap = (
+                lax.broadcasted_iota(jnp.int32, (size, rows), 1)
+                - lax.broadcasted_iota(jnp.int32, (size, rows), 0)
+                - first
+            )
+            line = jnp.where((gap <= 0) & (gap >= -2 * width), line, 0.0)
+            across_ref[s, first : first + size] = line.astype(across_ref.dtype)
+
+
+def plus(a, b):
+    return (a.astype(jnp.float32) + b.astype(jnp.float32)).astype(a.dtype)
 
 
 def position_of(values, wanted):
@@ -104,8 +120,6 @@
     wide,
     product,
     load_sem,
-    halo_send,
-    halo_recv,
     strip_send,
     strip_recv,
     facet_send,
@@ -117,6 +131,7 @@
 ):
     corr, scales, rows, side = x_ref.shape
     width = (taps_ref.shape[1] - 1) // 2
+    tall = rows + 2 * width
     tiles = side // COL_TILE
     contrib = fcols.shape[2]
     sub_side = fcols.shape[1]
@@ -126,12 +141,13 @@
     capacity = observed.shape[0] // devices
     sub_cols = col_taper.shape[0]
     sub_rows = row_taper.shape[0]
+    r_blocks, q_blocks = sub_side // LANES, sub_side // ALIGN
     f_me = lax.axis_index("facet")
     s_me = lax.axis_index("strip")
     me = f_me * n_strip + s_me
 
     x_loads = [
-        pltpu.make_async_copy(x_ref.at[c], x_buf.at[c, :, pl.ds(width, rows)], load_sem.at[c])
+        pltpu.make_async_copy(x_ref.at[c], x_buf.at[c], load_sem.at[c])
         for c in range(corr)
     ]
     others = [
@@ -174,58 +190,23 @@
             barrier, inc=1, device_id={"facet": lax.rem(f_me + off, n_facet)}, device_id_type=MESH
         )
     fill_bands(taps_ref, pad_ref, across_ref, down_ref, width)
-    y_ref[:, :, 0:LANES] = jnp.zeros((scales, rows, LANES), y_ref.dtype)
-    y_ref[:, :, LANES + side : 2 * LANES + side] = jnp.zeros((scales, rows, LANES), y_ref.dtype)
-    pl.semaphore_wait(barrier, n_strip + n_facet - 2)
-    right, left = lax.rem(s_me + 1, n_strip), lax.rem(s_me + n_strip - 1, n_strip)
-    halos = []
-    for c in range(corr):
-        pair = []
-        for way, (start, landing, peer) in enumerate(
-            ((rows - width, 0, right), (0, rows + width, left))
-        ):
-            copy = pltpu.make_async_remote_copy(
-                src_ref=x_ref.at[c, :, pl.ds(start, width)],
-                dst_ref=x_buf.at[c, :, pl.ds(landing, width)],
-                send_sem=halo_send.at[c, way],
-                recv_sem=halo_recv.at[c, way],
-                device_id={"strip": peer},
-                device_id_type=MESH,
-            )
-            copy.start()
-            pair.append(copy)
-        halos.append(pair)
-    for off in range(1, n_strip):
-        pl.semaphore_signal(
-            ready_sem, inc=1, device_id={"strip": lax.rem(s_me + off, n_strip)}, device_id_type=MESH
-        )
+    y_ref[:, :, 0:LANES] = jnp.zeros((scales, tall, LANES), y_ref.dtype)
+    y_ref[:, :, LANES + side : 2 * LANES + side] = jnp.zeros((scales, tall, LANES), y_ref.dtype)
     col_perm = [lax.rem(owner_ref[b], n_strip) for b in range(sub_cols)]
     row_perm = [lax.div(owner_ref[a * sub_cols], n_strip) for a in range(sub_rows)]
 
     strip_copies = []
     for c in range(corr):
         x_loads[c].wait()
-        for copy in halos[c]:
-            copy.wait()
-
-        @pl.when(s_me == 0)
-        def _():
-            x_buf[c, :, 0:width] = jnp.zeros((scales, width, side), x_buf.dtype)
-
-        @pl.when(s_me == n_strip - 1)
-        def _():
-            x_buf[c, :, rows + width : rows + 2 * width] = jnp.zeros((scales, width, side), x_buf.dtype)
-
         for s in range(scales):
-            for b in range(rows // LANES):
-                part = x_buf[c, s, b * LANES : (b + 1) * LANES + 2 * width]
-                y_ref[s, b * LANES : (b + 1) * LANES, LANES : LANES + side] = mm(
-                    across_ref[s], part
+            for n in range(0, side, COL_TILE):
+                y_ref[s, :, LANES + n : LANES + n + COL_TILE] = mm(
+                    across_ref[s], x_buf[c, s, :, n : n + COL_TILE]
                 ).astype(y_ref.dtype)
 
         def one_tile(tile, carry):
             first = pl.multiple_of(tile * COL_TILE, COL_TILE)
-            smoothed = jnp.zeros((rows, COL_TILE), jnp.float32)
+            smoothed = jnp.zeros((tall, COL_TILE), jnp.float32)
             for s in range(scales):
                 smoothed += mm(y_ref[s, :, pl.ds(first, COL_TILE + 2 * LANES)], down_ref[s])
             smooth_ref[:, pl.ds(first, COL_TILE)] = smoothed.astype(smooth_ref.dtype)
@@ -235,41 +216,36 @@
         if c == 0:
             for load in col_loads:
                 load.wait()
-        for off in range(1, n_strip + 1):
-            peer = lax.rem(s_me + off, n_strip)
-            b = position_of(col_perm, peer)
-            got = mm(smooth_ref[...], col_taper[b]).astype(stage.dtype)
-            if off == n_strip:
-                grouped[s_me, c] = got
-                continue
-            stage[c, off] = got
-            copy = pltpu.make_async_remote_copy(
-                src_ref=stage.at[c, off],
-                dst_ref=grouped.at[s_me, c],
-                send_sem=strip_send.at[c, off],
-                recv_sem=strip_recv.at[c, off],
-                device_id={"strip": peer},
-                device_id_type=MESH,
-            )
-            copy.start()
-            strip_copies.append(copy)
-
-    index_load.wait()
-    for c in range(corr):
-        row = gains_ref[c : c + 1, :]
-        product[c] = looked_up(row, index[:, 0, :]) * looked_up(row, index[:, 1, :])
-    dest = dest_ref[...]
-    k_row = lax.broadcasted_iota(jnp.int32, (blocks, blocks), 0)
-    k_col = lax.broadcasted_iota(jnp.int32, (blocks, blocks), 1)
-    dest_wide = jnp.broadcast_to(dest, (blocks, blocks))
-    dest_tall = jnp.sum(jnp.where(k_row == k_col, dest_wide, 0), axis=1, keepdims=True)
-    same = (dest_tall == dest_wide) & (k_row < k_col)
-    rank = jnp.sum(jnp.where(same, 1, 0), axis=0, keepdims=True)
-    target = dest * capacity + rank
-    code = jnp.concatenate([target * corr + c for c in range(corr)], axis=1)
-    places = lax.broadcasted_iota(jnp.int32, onehot.shape, 0)
-    onehot[...] = jnp.where(places == code, 1.0, 0.0).astype(onehot.dtype)
-    r_blocks, q_blocks = sub_side // LANES, sub_side // ALIGN
+            pl.semaphore_wait(barrier, n_strip + n_facet - 2)
+            for off in range(1, n_strip):
+                pl.semaphore_signal(
+                    ready_sem,
+                    inc=1,
+                    device_id={"strip": lax.rem(s_me + off, n_strip)},
+                    device_id_type=MESH,
+                )
+        for first in range(1, n_strip + 1, 2):
+            peers = [lax.rem(s_me + off, n_strip) for off in (first, first + 1)]
+            pair = jnp.concatenate([col_taper[position_of(col_perm, peer)] for peer in peers], axis=1)
+            got = mm(smooth_ref[...], pair).astype(stage.dtype)
+            for n, peer in enumerate(peers):
+                off = first + n
+                part = got[:, n * contrib : (n + 1) * contrib]
+                if off == n_strip:
+                    grouped[s_me, c] = part
+                    continue
+                stage[c, off] = part
+                copy = pltpu.make_async_remote_copy(
+                    src_ref=stage.at[c, off],
+                    dst_ref=grouped.at[s_me, c],
+                    send_sem=strip_send.at[c, off],
+                    recv_sem=strip_recv.at[c, off],
+                    device_id={"strip": peer},
+                    device_id_type=MESH,
+                )
+                copy.start()
+                strip_copies.append(copy)
+
     turned[:, r_blocks] = jnp.zeros((corr,) + turned.shape[2:], turned.dtype)
     turned[:, :, q_blocks] = jnp.zeros((corr, r_blocks + 1, ALIGN, LANES), turned.dtype)
     offset_load.wait()
@@ -303,30 +279,43 @@
         load.wait()
 
     facet_copies = []
-    for c in range(corr):
+
+    def contribute(c):
         for copy in strip_copies[c * (n_strip - 1) : (c + 1) * (n_strip - 1)]:
             copy.wait()
-        flipped = jnp.concatenate([grouped[x, c].T for x in range(n_strip)], axis=1)
-        for off in range(1, n_facet + 1):
-            peer = lax.rem(f_me + off, n_facet)
-            a = position_of(row_perm, peer)
-            got = mm(flipped, row_taper[a]).astype(stage2.dtype)
-            if off == n_facet:
-                mine[f_me, c] = got
-                continue
-            stage2[c, off] = got
-            copy = pltpu.make_async_remote_copy(
-                src_ref=stage2.at[c, off],
-                dst_ref=mine.at[f_me, c],
-                send_sem=facet_send.at[c, off],
-                recv_sem=facet_recv.at[c, off],
-                device_id={"facet": peer},
-                device_id_type=MESH,
-            )
-            copy.start()
-            facet_copies.append(copy)
-
-    for c in range(corr):
+        flipped = []
+        for x in range(n_strip):
+            top, bottom = grouped[x, c, width : 2 * width], grouped[x, c, rows : rows + width]
+            if x > 0:
+                top = plus(top, grouped[x - 1, c, rows + width : rows + 2 * width])
+            if x < n_strip - 1:
+                bottom = plus(bottom, grouped[x + 1, c, 0:width])
+            block = jnp.concatenate([top, grouped[x, c, 2 * width : rows], bottom], axis=0)
+            flipped.append(block.T)
+        flipped = jnp.concatenate(flipped, axis=1)
+        for first in range(1, n_facet + 1, 2):
+            peers = [lax.rem(f_me + off, n_facet) for off in (first, first + 1)]
+            pair = jnp.concatenate([row_taper[position_of(row_perm, peer)] for peer in peers], axis=1)
+            got = mm(flipped, pair).astype(stage2.dtype)
+            for n, peer in enumerate(peers):
+                off = first + n
+                part = got[:, n * contrib : (n + 1) * contrib]
+                if off == n_facet:
+                    mine[f_me, c] = part
+                    continue
+                stage2[c, off] = part
+                copy = pltpu.make_async_remote_copy(
+                    src_ref=stage2.at[c, off],
+                    dst_ref=mine.at[f_me, c],
+                    send_sem=facet_send.at[c, off],
+                    recv_sem=facet_recv.at[c, off],
+                    device_id={"facet": peer},
+                    device_id_type=MESH,
+                )
+                copy.start()
+                facet_copies.append(copy)
+
+    def degrid(c):
         for copy in facet_copies[c * (n_facet - 1) : (c + 1) * (n_facet - 1)]:
             copy.wait()
         for f in range(n_facet):
@@ -343,7 +332,7 @@
                 .reshape(q_blocks, ALIGN, LANES)
             )
 
-        def one_block(k, carry, c=c):
+        def one_block(k, carry):
             _, _, rb, qb = corner(k)
             tile = jnp.concatenate(
                 [
@@ -358,6 +347,29 @@
 
         lax.fori_loop(0, blocks, one_block, 0, unroll=8)
 
+    contribute(0)
+    for c in range(corr):
+        if c + 1 < corr:
+            degrid(c)
+            contribute(c + 1)
+            continue
+        index_load.wait()
+        for n in range(corr):
+            row = gains_ref[n : n + 1, :]
+            product[n] = looked_up(row, index[:, 0, :]) * looked_up(row, index[:, 1, :])
+        dest = dest_ref[...]
+        k_row = lax.broadcasted_iota(jnp.int32, (blocks, blocks), 0)
+        k_col = lax.broadcasted_iota(jnp.int32, (blocks, blocks), 1)
+        dest_wide = jnp.broadcast_to(dest, (blocks, blocks))
+        dest_tall = jnp.sum(jnp.where(k_row == k_col, dest_wide, 0), axis=1, keepdims=True)
+        same = (dest_tall == dest_wide) & (k_row < k_col)
+        rank = jnp.sum(jnp.where(same, 1, 0), axis=0, keepdims=True)
+        target = dest * capacity + rank
+        code = jnp.concatenate([target * corr + n for n in range(corr)], axis=1)
+        places = lax.broadcasted_iota(jnp.int32, onehot.shape, 0)
+        onehot[...] = jnp.where(places == code, 1.0, 0.0).astype(onehot.dtype)
+        degrid(c)
+
     outgoing[...] = (
         mm(onehot[...], values[...].astype(jnp.bfloat16))
         .astype(outgoing.dtype)
@@ -365,22 +377,24 @@
     )
     pl.semaphore_wait(ready_sem, n_strip - 1)
 
-    def vis_copy(off):
-        peer = lax.rem(me + off, devices)
-        return pltpu.make_async_remote_copy(
-            src_ref=outgoing.at[peer],
-            dst_ref=arrived.at[me],
-            send_sem=vis_send.at[off],
-            recv_sem=vis_recv.at[off],
-            device_id={"facet": peer // n_strip, "strip": peer % n_strip},
-            device_id_type=MESH,
-        )
-
-    def send_one(off, carry):
-        vis_copy(off).start()
-        return carry
-
-    lax.fori_loop(1, devices, send_one, 0)
+    vis_copies = []
+    for f_off in [n_facet // 2] + [n for n in range(n_facet) if n != n_facet // 2]:
+        f_peer = lax.rem(f_me + f_off, n_facet)
+        for s_off in range(n_strip):
+            if f_off == 0 and s_off == 0:
+                continue
+            s_peer = lax.rem(s_me + s_off, n_strip)
+            off = f_off * n_strip + s_off
+            copy = pltpu.make_async_remote_copy(
+                src_ref=outgoing.at[f_peer * n_strip + s_peer],
+                dst_ref=arrived.at[me],
+                send_sem=vis_send.at[off],
+                recv_sem=vis_recv.at[off],
+                device_id={"facet": f_peer, "strip": s_peer},
+                device_id_type=MESH,
+            )
+            copy.start()
+            vis_copies.append(copy)
     arrived[me] = outgoing[me]
     subgrid_copies = []
     for c in range(corr):
@@ -392,17 +406,52 @@
         subgrid_copies.append(copy)
     observed_load.wait()
 
-    def wait_one(off, carry):
-        vis_copy(off).wait()
-        return carry
-
-    lax.fori_loop(1, devices, wait_one, 0)
+    for copy in vis_copies:
+        copy.wait()
     wide[...] = arrived[...].astype(jnp.float32).reshape(wide.shape)
     for c in range(corr):
         placed = wide[pl.ds(c, devices * capacity, stride=corr), :]
         residual_out[:, c, :] = observed[:, c, :] - product[c] * placed
     for copy in subgrid_copies:
         copy.wait()
+
+
+def pass_kernel(a_ref, b_ref, a_out, b_out, a_buf, b_buf, in_sem, out_sem):
+    parts = a_ref.shape[0]
+    pairs = [(a_ref.at[n], a_buf.at[n], a_out.at[n]) for n in range(parts)]
+    pairs.append((b_ref, b_buf, b_out))
+    loads = [pltpu.make_async_copy(src, buf, in_sem.at[n]) for n, (src, buf, _) in enumerate(pairs)]
+    stores = [pltpu.make_async_copy(buf, dst, out_sem.at[n]) for n, (_, buf, dst) in enumerate(pairs)]
+    for load in loads:
+        load.start()
+    for load, store in zip(loads, stores):
+        load.wait()
+        store.start()
+    for store in stores:
+        store.wait()
+
+
+def handed_on(subgrid, residual):
+    parts = 8
+    cut = subgrid.reshape(parts, -1, subgrid.shape[-1])
+    remote = pl.BlockSpec(memory_space=pl.ANY)
+    a, b = pl.pallas_call(
+        pass_kernel,
+        in_specs=[remote, remote],
+        out_specs=[remote, remote],
+        out_shape=[
+            jax.ShapeDtypeStruct(cut.shape, cut.dtype),
+            jax.ShapeDtypeStruct(residual.shape, residual.dtype),
+        ],
+        scratch_shapes=[
+            pltpu.VMEM(cut.shape, cut.dtype),
+            pltpu.VMEM(residual.shape, residual.dtype),
+            pltpu.SemaphoreType.DMA((parts + 1,)),
+            pltpu.SemaphoreType.DMA((parts + 1,)),
+        ],
+        name="handed_on",
+    )(cut, residual)
+    return a.reshape(subgrid.shape), b
 
 
 def on_device(
@@ -425,7 +474,7 @@
     devices = n_facet * n_strip
     comp = sky_components[0]
     corr, scales, rows, side = comp.shape
-    taps = scale_kernels.shape[1]
+    tall = rows + scale_kernels.shape[1] - 1
     sub_side, contrib = finish_cols.shape[1], finish_cols.shape[2]
     blocks, _, vis = vis_offset.shape
     sub_rows, sub_cols = row_taper.shape[2] // contrib, col_taper.shape[2] // contrib
@@ -445,7 +494,7 @@
             jax.ShapeDtypeStruct(observed.shape, f32),
         ],
         scratch_shapes=[
-            pltpu.VMEM((corr, scales, rows + taps - 1, side), bf16),
+            pltpu.VMEM((corr, scales, rows, side), bf16),
             pltpu.VMEM((sub_cols, side, contrib), bf16),
             pltpu.VMEM((sub_rows, side, contrib), bf16),
             pltpu.VMEM(finish_rows.shape, bf16),
@@ -454,12 +503,12 @@
             pltpu.VMEM(antenna_pair_index.shape, jnp.int32),
             pltpu.VMEM(observed.shape, f32),
             pltpu.VMEM((scales, 2 * LANES), f32),
-            pltpu.VMEM((scales, LANES, LANES + taps - 1), bf16),
+            pltpu.VMEM((scales, tall, rows), bf16),
             pltpu.VMEM((scales, COL_TILE + 2 * LANES, COL_TILE), bf16),
-            pltpu.VMEM((scales, rows, side + 2 * LANES), bf16),
-            pltpu.VMEM((rows, side), bf16),
-            pltpu.VMEM((corr, n_strip, rows, contrib), bf16),
-            pltpu.VMEM((n_strip, corr, rows, contrib), bf16),
+            pltpu.VMEM((scales, tall, side + 2 * LANES), bf16),
+            pltpu.VMEM((tall, side), bf16),
+            pltpu.VMEM((corr, n_strip, tall, contrib), bf16),
+            pltpu.VMEM((n_strip, corr, tall, contrib), bf16),
             pltpu.VMEM((corr, n_facet, contrib, contrib), bf16),
             pltpu.VMEM((n_facet, corr, contrib, contrib), bf16),
             pltpu.VMEM((sub_side, n_facet * contrib), bf16),
@@ -475,8 +524,6 @@
             pltpu.VMEM((devices * per_device, vis), f32),
             pltpu.VMEM((corr, slots, vis), f32),
             dma((corr + 5 + sub_cols + sub_rows,)),
-            dma((corr, 2)),
-            dma((corr, 2)),
             dma((corr, n_strip)),
             dma((corr, n_strip)),
             dma((corr, n_facet)),
@@ -505,6 +552,7 @@
         antenna_pair_index,
         observed,
     )
+    subgrid, residual = handed_on(subgrid, residual)
     return subgrid[None], residual
 
 

time: 59.7 us -> 50.6 us (0.85)
  Pallas kernels: 55 us -> 49.8 us
  local copies, waits for them, and re-layouts: 3.83 us -> 0 us
    pallas_call x1, Pallas kernels: 55 us -> 47.6 us  [on_device(): pl.pallas_call(functools.partial(whole_kernel, n_facet, n_strip), in_spec...]
    unnamed x2 -> x0, local copies, waits for them, and re-layouts: 3.83 us -> none
    pallas_call x0 -> x1, Pallas kernels: none -> 2.15 us  [handed_on(): pl.pallas_call(pass_kernel, in_specs=[remote, remote], out_specs=[remote,...]
where the time goes in v2:
time: 50.6 us; the launch traced here: 50.4 us
  Pallas kernels  49.8 us (98%)
  between operations  0.64 us (1%)
    pallas_call x1, Pallas kernels, on_device(): pl.pallas_call(functools.partial(whole_kernel, n_facet, n_strip), in_spec...  47.6 us
    pallas_call x1, Pallas kernels, handed_on(): pl.pallas_call(pass_kernel, in_specs=[remote, remote], out_specs=[remote,...  2.15 us

profile of v2, /device:TPU:0, one launch (start us, length us, event | category | flops | bytes accessed | tf_op | source)
XLA Modules:
  0.0 50.4 jit_solution(8424249930233550104)
XLA Ops:
  0.6 47.6 %sky_to_residual.1 = (bf16[2,512,512]{2,1,0:T(8,128)(2,1)}, f32[128,2,128]{2,1,0:T(2,128)}) custom-call(s32[32]{0:T(128)} %owner_ref.1, s32[2,64]{1,0:T(2,128)} %bitcast.11, f32[4,33]{1,0:T(4,128)} %taps_ref.1, s32[1,64]{1,0:T(1,128)} %bitcast.12, f32[2,512]{1,0:T(2,128)} %gains_ref.1, bf16[2,4,256,2048]{3,2,1,0:T(8,128)(2,1)} %bitcast.7, ...), custom_call_target="tpu_custom_call" | custom-call | tf_op jit(solution)/shard_map/sky_to_residual/pallas_call | solution.py:488
  48.2 2.1 %handed_on.1 = (bf16[8,128,512]{2,1,0:T(8,128)(2,1)}, f32[128,2,128]{2,1,0:T(2,128)}) custom-call(bf16[8,128,512]{2,1,0:T(8,128)(2,1)} %bitcast.10, f32[128,2,128]{2,1,0:T(2,128)} %get-tuple-element.7.b_ref), custom_call_target="tpu_custom_call" | custom-call | tf_op jit(solution)/shard_map/handed_on/pallas_call | solution.py:438

commit v3 on v2

--- a/solution.py
+++ b/solution.py
@@ -22,9 +22,18 @@
     return jnp.dot(a, b, preferred_element_type=jnp.float32)
 
 
-def fill_bands(taps_ref, pad_ref, across_ref, down_ref, width):
+def row_chunks(rows, width):
+    count = rows // LANES
+    chunks = []
+    for h in range(count):
+        low = h * LANES if h else -width
+        high = (h + 1) * LANES if h < count - 1 else rows + width
+        chunks.append((low, high, max(0, low - width), min(rows, high + width)))
+    return chunks
+
+
+def fill_bands(taps_ref, pad_ref, across_ref, down_ref, width, chunks):
     scales, taps = taps_ref.shape
-    tall, rows = across_ref.shape[1:]
     span = LANES + taps - 1
     pad_ref[...] = jnp.zeros_like(pad_ref)
     pad_ref[:, 0:taps] = taps_ref[...]
@@ -36,18 +45,17 @@
         for tile in range(COL_TILE // LANES):
             start = LANES - width + tile * LANES
             down_ref[s, start : start + span, tile * LANES : (tile + 1) * LANES] = down
-        for first in range(0, tall, LANES):
-            size = min(LANES, tall - first)
-            line = jnp.broadcast_to(pad_ref[s : s + 1, 0:rows], (size, rows))
-            line = pltpu.roll(line, (rows + first - 2 * width) % rows, 1)
-            line = pltpu.roll(line, 0, 1, stride=1, stride_axis=0)
-            gap = (
-                lax.broadcasted_iota(jnp.int32, (size, rows), 1)
-                - lax.broadcasted_iota(jnp.int32, (size, rows), 0)
-                - first
-            )
-            line = jnp.where((gap <= 0) & (gap >= -2 * width), line, 0.0)
-            across_ref[s, first : first + size] = line.astype(across_ref.dtype)
+        for h, (low, high, x_low, x_high) in enumerate(chunks):
+            for first in range(0, high - low, LANES):
+                size = min(LANES, high - low - first)
+                line = jnp.broadcast_to(pad_ref[s : s + 1, :], (size, 2 * LANES))
+                shift = (low - width - x_low + first) % (2 * LANES)
+                if shift:
+                    line = pltpu.roll(line, shift, 1)
+                line = pltpu.roll(line, 0, 1, stride=1, stride_axis=0)
+                across_ref[h, s, first : first + size] = line[:, 0 : x_high - x_low].astype(
+                    across_ref.dtype
+                )
 
 
 def plus(a, b):
@@ -131,7 +139,9 @@
 ):
     corr, scales, rows, side = x_ref.shape
     width = (taps_ref.shape[1] - 1) // 2
-    tall = rows + 2 * width
+    chunks = row_chunks(rows, width)
+    n_chunk = len(chunks)
+    tall = chunks[0][1] - chunks[0][0]
     tiles = side // COL_TILE
     contrib = fcols.shape[2]
     sub_side = fcols.shape[1]
@@ -146,12 +156,19 @@
     s_me = lax.axis_index("strip")
     me = f_me * n_strip + s_me
 
-    x_loads = [
-        pltpu.make_async_copy(x_ref.at[c], x_buf.at[c], load_sem.at[c])
-        for c in range(corr)
-    ]
+    x_loads = []
+    for c in range(corr):
+        x_low = 0
+        for h, (_, _, _, x_high) in enumerate(chunks):
+            part = pl.ds(x_low, x_high - x_low)
+            x_loads.append(
+                pltpu.make_async_copy(
+                    x_ref.at[c, :, part], x_buf.at[c, :, part], load_sem.at[c * n_chunk + h]
+                )
+            )
+            x_low = x_high
     others = [
-        pltpu.make_async_copy(src, dst, load_sem.at[corr + n])
+        pltpu.make_async_copy(src, dst, load_sem.at[corr * n_chunk + n])
         for n, (src, dst) in enumerate(
             (
                 (index_in, index),
@@ -165,7 +182,7 @@
     index_load, offset_load, frows_load, fcols_load, observed_load = others
     col_loads = [
         pltpu.make_async_copy(
-            col_in.at[:, pl.ds(b * contrib, contrib)], col_taper.at[b], load_sem.at[corr + 5 + b]
+            col_in.at[:, pl.ds(b * contrib, contrib)], col_taper.at[b], load_sem.at[corr * n_chunk + 5 + b]
         )
         for b in range(sub_cols)
     ]
@@ -173,11 +190,11 @@
         pltpu.make_async_copy(
             row_in.at[:, pl.ds(a * contrib, contrib)],
             row_taper.at[a],
-            load_sem.at[corr + 5 + sub_cols + a],
+            load_sem.at[corr * n_chunk + 5 + sub_cols + a],
         )
         for a in range(sub_rows)
     ]
-    for load in x_loads + col_loads + others + row_loads:
+    for load in x_loads[:n_chunk] + col_loads + x_loads[n_chunk:] + others + row_loads:
         load.start()
 
     barrier = pltpu.get_barrier_semaphore()
@@ -189,19 +206,21 @@
         pl.semaphore_signal(
             barrier, inc=1, device_id={"facet": lax.rem(f_me + off, n_facet)}, device_id_type=MESH
         )
-    fill_bands(taps_ref, pad_ref, across_ref, down_ref, width)
+    fill_bands(taps_ref, pad_ref, across_ref, down_ref, width, chunks)
     y_ref[:, :, 0:LANES] = jnp.zeros((scales, tall, LANES), y_ref.dtype)
     y_ref[:, :, LANES + side : 2 * LANES + side] = jnp.zeros((scales, tall, LANES), y_ref.dtype)
     col_perm = [lax.rem(owner_ref[b], n_strip) for b in range(sub_cols)]
     row_perm = [lax.div(owner_ref[a * sub_cols], n_strip) for a in range(sub_rows)]
 
     strip_copies = []
-    for c in range(corr):
-        x_loads[c].wait()
+    for n_part in range(corr * n_chunk):
+        c, h = divmod(n_part, n_chunk)
+        low, high, x_low, x_high = chunks[h]
+        x_loads[n_part].wait()
         for s in range(scales):
             for n in range(0, side, COL_TILE):
                 y_ref[s, :, LANES + n : LANES + n + COL_TILE] = mm(
-                    across_ref[s], x_buf[c, s, :, n : n + COL_TILE]
+                    across_ref[h, s], x_buf[c, s, x_low:x_high, n : n + COL_TILE]
                 ).astype(y_ref.dtype)
 
         def one_tile(tile, carry):
@@ -212,8 +231,8 @@
             smooth_ref[:, pl.ds(first, COL_TILE)] = smoothed.astype(smooth_ref.dtype)
             return carry
 
-        lax.fori_loop(0, tiles, one_tile, 0, unroll=2)
-        if c == 0:
+        lax.fori_loop(0, tiles, one_tile, 0, unroll=4)
+        if n_part == 0:
             for load in col_loads:
                 load.wait()
             pl.semaphore_wait(barrier, n_strip + n_facet - 2)
@@ -232,14 +251,14 @@
                 off = first + n
                 part = got[:, n * contrib : (n + 1) * contrib]
                 if off == n_strip:
-                    grouped[s_me, c] = part
+                    grouped[s_me, n_part] = part
                     continue
-                stage[c, off] = part
+                stage[n_part, off] = part
                 copy = pltpu.make_async_remote_copy(
-                    src_ref=stage.at[c, off],
-                    dst_ref=grouped.at[s_me, c],
-                    send_sem=strip_send.at[c, off],
-                    recv_sem=strip_recv.at[c, off],
+                    src_ref=stage.at[n_part, off],
+                    dst_ref=grouped.at[s_me, n_part],
+                    send_sem=strip_send.at[n_part, off],
+                    recv_sem=strip_recv.at[n_part, off],
                     device_id={"strip": peer},
                     device_id_type=MESH,
                 )
@@ -281,16 +300,24 @@
     facet_copies = []
 
     def contribute(c):
-        for copy in strip_copies[c * (n_strip - 1) : (c + 1) * (n_strip - 1)]:
+        each = n_chunk * (n_strip - 1)
+        for copy in strip_copies[c * each : (c + 1) * each]:
             copy.wait()
+        head, tail = c * n_chunk, (c + 1) * n_chunk - 1
         flipped = []
         for x in range(n_strip):
-            top, bottom = grouped[x, c, width : 2 * width], grouped[x, c, rows : rows + width]
+            top = grouped[x, head, width : 2 * width]
+            bottom = grouped[x, tail, tall - 2 * width : tall - width]
             if x > 0:
-                top = plus(top, grouped[x - 1, c, rows + width : rows + 2 * width])
+                top = plus(top, grouped[x - 1, tail, tall - width : tall])
             if x < n_strip - 1:
-                bottom = plus(bottom, grouped[x + 1, c, 0:width])
-            block = jnp.concatenate([top, grouped[x, c, 2 * width : rows], bottom], axis=0)
+                bottom = plus(bottom, grouped[x + 1, head, 0:width])
+            middle = []
+            for n_part in range(head, tail + 1):
+                start = 2 * width if n_part == head else 0
+                stop = tall - 2 * width if n_part == tail else tall
+                middle.append(grouped[x, n_part, start:stop])
+            block = jnp.concatenate([top] + middle + [bottom], axis=0)
             flipped.append(block.T)
         flipped = jnp.concatenate(flipped, axis=1)
         for first in range(1, n_facet + 1, 2):
@@ -348,27 +375,25 @@
         lax.fori_loop(0, blocks, one_block, 0, unroll=8)
 
     contribute(0)
-    for c in range(corr):
-        if c + 1 < corr:
-            degrid(c)
-            contribute(c + 1)
-            continue
-        index_load.wait()
-        for n in range(corr):
-            row = gains_ref[n : n + 1, :]
-            product[n] = looked_up(row, index[:, 0, :]) * looked_up(row, index[:, 1, :])
-        dest = dest_ref[...]
-        k_row = lax.broadcasted_iota(jnp.int32, (blocks, blocks), 0)
-        k_col = lax.broadcasted_iota(jnp.int32, (blocks, blocks), 1)
-        dest_wide = jnp.broadcast_to(dest, (blocks, blocks))
-        dest_tall = jnp.sum(jnp.where(k_row == k_col, dest_wide, 0), axis=1, keepdims=True)
-        same = (dest_tall == dest_wide) & (k_row < k_col)
-        rank = jnp.sum(jnp.where(same, 1, 0), axis=0, keepdims=True)
-        target = dest * capacity + rank
-        code = jnp.concatenate([target * corr + n for n in range(corr)], axis=1)
-        places = lax.broadcasted_iota(jnp.int32, onehot.shape, 0)
-        onehot[...] = jnp.where(places == code, 1.0, 0.0).astype(onehot.dtype)
-        degrid(c)
+    index_load.wait()
+    for n in range(corr):
+        row = gains_ref[n : n + 1, :]
+        product[n] = looked_up(row, index[:, 0, :]) * looked_up(row, index[:, 1, :])
+    dest = dest_ref[...]
+    k_row = lax.broadcasted_iota(jnp.int32, (blocks, blocks), 0)
+    k_col = lax.broadcasted_iota(jnp.int32, (blocks, blocks), 1)
+    dest_wide = jnp.broadcast_to(dest, (blocks, blocks))
+    dest_tall = jnp.sum(jnp.where(k_row == k_col, dest_wide, 0), axis=1, keepdims=True)
+    same = (dest_tall == dest_wide) & (k_row < k_col)
+    rank = jnp.sum(jnp.where(same, 1, 0), axis=0, keepdims=True)
+    target = dest * capacity + rank
+    code = jnp.concatenate([target * corr + n for n in range(corr)], axis=1)
+    places = lax.broadcasted_iota(jnp.int32, onehot.shape, 0)
+    onehot[...] = jnp.where(places == code, 1.0, 0.0).astype(onehot.dtype)
+    for c in range(1, corr):
+        contribute(c)
+        degrid(c - 1)
+    degrid(corr - 1)
 
     outgoing[...] = (
         mm(onehot[...], values[...].astype(jnp.bfloat16))
@@ -474,7 +499,9 @@
     devices = n_facet * n_strip
     comp = sky_components[0]
     corr, scales, rows, side = comp.shape
-    tall = rows + scale_kernels.shape[1] - 1
+    chunks = row_chunks(rows, (scale_kernels.shape[1] - 1) // 2)
+    n_chunk = len(chunks)
+    tall = chunks[0][1] - chunks[0][0]
     sub_side, contrib = finish_cols.shape[1], finish_cols.shape[2]
     blocks, _, vis = vis_offset.shape
     sub_rows, sub_cols = row_taper.shape[2] // contrib, col_taper.shape[2] // contrib
@@ -503,12 +530,12 @@
             pltpu.VMEM(antenna_pair_index.shape, jnp.int32),
             pltpu.VMEM(observed.shape, f32),
             pltpu.VMEM((scales, 2 * LANES), f32),
-            pltpu.VMEM((scales, tall, rows), bf16),
+            pltpu.VMEM((n_chunk, scales, tall, chunks[0][3] - chunks[0][2]), bf16),
             pltpu.VMEM((scales, COL_TILE + 2 * LANES, COL_TILE), bf16),
             pltpu.VMEM((scales, tall, side + 2 * LANES), bf16),
             pltpu.VMEM((tall, side), bf16),
-            pltpu.VMEM((corr, n_strip, tall, contrib), bf16),
-            pltpu.VMEM((n_strip, corr, tall, contrib), bf16),
+            pltpu.VMEM((corr * n_chunk, n_strip, tall, contrib), bf16),
+            pltpu.VMEM((n_strip, corr * n_chunk, tall, contrib), bf16),
             pltpu.VMEM((corr, n_facet, contrib, contrib), bf16),
             pltpu.VMEM((n_facet, corr, contrib, contrib), bf16),
             pltpu.VMEM((sub_side, n_facet * contrib), bf16),
@@ -523,9 +550,9 @@
             pltpu.VMEM((devices, per_device, vis), bf16),
             pltpu.VMEM((devices * per_device, vis), f32),
             pltpu.VMEM((corr, slots, vis), f32),
-            dma((corr + 5 + sub_cols + sub_rows,)),
-            dma((corr, n_strip)),
-            dma((corr, n_strip)),
+            dma((corr * n_chunk + 5 + sub_cols + sub_rows,)),
+            dma((corr * n_chunk, n_strip)),
+            dma((corr * n_chunk, n_strip)),
             dma((corr, n_facet)),
             dma((corr, n_facet)),
             dma((devices,)),

time: 50.6 us -> 48.3 us (0.955)
  Pallas kernels: 49.8 us -> 47.3 us
    pallas_call x1, Pallas kernels: 47.6 us -> 45.1 us  [on_device(): pl.pallas_call(functools.partial(whole_kernel, n_facet, n_strip), in_spec...]
where the time goes in v3:
time: 48.3 us; the launch traced here: 48.1 us
  Pallas kernels  47.3 us (98%)
  between operations  0.8 us (2%)
    pallas_call x1, Pallas kernels, on_device(): pl.pallas_call(functools.partial(whole_kernel, n_facet, n_strip), in_spec...  45.1 us
    pallas_call x1, Pallas kernels, handed_on(): pl.pallas_call(pass_kernel, in_specs=[remote, remote], out_specs=[remote,...  2.15 us

profile of v3, /device:TPU:0, one launch (start us, length us, event | category | flops | bytes accessed | tf_op | source)
XLA Modules:
  0.0 48.1 jit_solution(4946140434196203440)
XLA Ops:
  0.6 45.1 %sky_to_residual.1 = (bf16[2,512,512]{2,1,0:T(8,128)(2,1)}, f32[128,2,128]{2,1,0:T(2,128)}) custom-call(s32[32]{0:T(128)} %owner_ref.1, s32[2,64]{1,0:T(2,128)} %bitcast.11, f32[4,33]{1,0:T(4,128)} %taps_ref.1, s32[1,64]{1,0:T(1,128)} %bitcast.12, f32[2,512]{1,0:T(2,128)} %gains_ref.1, bf16[2,4,256,2048]{3,2,1,0:T(8,128)(2,1)} %bitcast.7, ...), custom_call_target="tpu_custom_call" | custom-call | tf_op jit(solution)/shard_map/sky_to_residual/pallas_call | solution.py:515
  45.8 2.1 %handed_on.1 = (bf16[8,128,512]{2,1,0:T(8,128)(2,1)}, f32[128,2,128]{2,1,0:T(2,128)}) custom-call(bf16[8,128,512]{2,1,0:T(8,128)(2,1)} %bitcast.10, f32[128,2,128]{2,1,0:T(2,128)} %get-tuple-element.7.b_ref), custom_call_target="tpu_custom_call" | custom-call | tf_op jit(solution)/shard_map/handed_on/pallas_call | solution.py:463

commit v4 on v3

--- a/solution.py
+++ b/solution.py
@@ -68,6 +68,15 @@
         gap = value - wanted
         place += j * jnp.maximum(1 - gap * gap, 0)
     return jnp.minimum(place, len(values) - 1)
+
+
+def flipped_bits(place, mask, count):
+    bit, out = 1, 0
+    while bit < count:
+        held = lax.rem(lax.div(place, bit), 2)
+        out += bit * ((1 - held) if mask & bit else held)
+        bit *= 2
+    return out
 
 
 def looked_up(row, index):
@@ -162,13 +171,18 @@
         for h, (_, _, _, x_high) in enumerate(chunks):
             part = pl.ds(x_low, x_high - x_low)
             x_loads.append(
-                pltpu.make_async_copy(
-                    x_ref.at[c, :, part], x_buf.at[c, :, part], load_sem.at[c * n_chunk + h]
-                )
+                [
+                    pltpu.make_async_copy(
+                        x_ref.at[c, s, part],
+                        x_buf.at[c, s, part],
+                        load_sem.at[(c * n_chunk + h) * scales + s],
+                    )
+                    for s in range(scales)
+                ]
             )
             x_low = x_high
     others = [
-        pltpu.make_async_copy(src, dst, load_sem.at[corr * n_chunk + n])
+        pltpu.make_async_copy(src, dst, load_sem.at[corr * n_chunk * scales + n])
         for n, (src, dst) in enumerate(
             (
                 (index_in, index),
@@ -182,7 +196,7 @@
     index_load, offset_load, frows_load, fcols_load, observed_load = others
     col_loads = [
         pltpu.make_async_copy(
-            col_in.at[:, pl.ds(b * contrib, contrib)], col_taper.at[b], load_sem.at[corr * n_chunk + 5 + b]
+            col_in.at[:, pl.ds(b * contrib, contrib)], col_taper.at[b], load_sem.at[corr * n_chunk * scales + 5 + b]
         )
         for b in range(sub_cols)
     ]
@@ -190,11 +204,11 @@
         pltpu.make_async_copy(
             row_in.at[:, pl.ds(a * contrib, contrib)],
             row_taper.at[a],
-            load_sem.at[corr * n_chunk + 5 + sub_cols + a],
+            load_sem.at[corr * n_chunk * scales + 5 + sub_cols + a],
         )
         for a in range(sub_rows)
     ]
-    for load in x_loads[:n_chunk] + col_loads + x_loads[n_chunk:] + others + row_loads:
+    for load in x_loads[0]:
         load.start()
 
     barrier = pltpu.get_barrier_semaphore()
@@ -216,8 +230,14 @@
     for n_part in range(corr * n_chunk):
         c, h = divmod(n_part, n_chunk)
         low, high, x_low, x_high = chunks[h]
-        x_loads[n_part].wait()
         for s in range(scales):
+            x_loads[n_part][s].wait()
+            if s == scales - 1 and n_part == 0:
+                for load in col_loads + x_loads[1]:
+                    load.start()
+            if s == scales - 1 and n_part == 1:
+                for load in [load for part in x_loads[2:] for load in part] + others + row_loads:
+                    load.start()
             for n in range(0, side, COL_TILE):
                 y_ref[s, :, LANES + n : LANES + n + COL_TILE] = mm(
                     across_ref[h, s], x_buf[c, s, x_low:x_high, n : n + COL_TILE]
@@ -320,14 +340,14 @@
             block = jnp.concatenate([top] + middle + [bottom], axis=0)
             flipped.append(block.T)
         flipped = jnp.concatenate(flipped, axis=1)
-        for first in range(1, n_facet + 1, 2):
-            peers = [lax.rem(f_me + off, n_facet) for off in (first, first + 1)]
+        for first in range(n_facet - 1, 0, -2):
+            offs = (first, first - 1)
+            peers = [flipped_bits(f_me, off, n_facet) for off in offs]
             pair = jnp.concatenate([row_taper[position_of(row_perm, peer)] for peer in peers], axis=1)
             got = mm(flipped, pair).astype(stage2.dtype)
-            for n, peer in enumerate(peers):
-                off = first + n
+            for n, (off, peer) in enumerate(zip(offs, peers)):
                 part = got[:, n * contrib : (n + 1) * contrib]
-                if off == n_facet:
+                if off == 0:
                     mine[f_me, c] = part
                     continue
                 stage2[c, off] = part
@@ -550,7 +570,7 @@
             pltpu.VMEM((devices, per_device, vis), bf16),
             pltpu.VMEM((devices * per_device, vis), f32),
             pltpu.VMEM((corr, slots, vis), f32),
-            dma((corr * n_chunk + 5 + sub_cols + sub_rows,)),
+            dma((corr * n_chunk * scales + 5 + sub_cols + sub_rows,)),
             dma((corr * n_chunk, n_strip)),
             dma((corr * n_chunk, n_strip)),
             dma((corr, n_facet)),

time: 48.3 us -> 49.9 us (1.033)
  Pallas kernels: 47.3 us -> 48.9 us
    pallas_call x1, Pallas kernels: 45.1 us -> 46.7 us  [on_device(): pl.pallas_call(functools.partial(whole_kernel, n_facet, n_strip), in_spec...]
where the time goes in v4:
time: 49.9 us; the launch traced here: 49.7 us
  Pallas kernels  48.9 us (98%)
  between operations  0.8 us (2%)
    pallas_call x1, Pallas kernels, on_device(): pl.pallas_call(functools.partial(whole_kernel, n_facet, n_strip), in_spec...  46.7 us
    pallas_call x1, Pallas kernels, handed_on(): pl.pallas_call(pass_kernel, in_specs=[remote, remote], out_specs=[remote,...  2.15 us

profile of v4, /device:TPU:0, one launch (start us, length us, event | category | flops | bytes accessed | tf_op | source)
XLA Modules:
  0.0 49.7 jit_solution(3427261994550875106)
XLA Ops:
  0.6 46.7 %sky_to_residual.1 = (bf16[2,512,512]{2,1,0:T(8,128)(2,1)}, f32[128,2,128]{2,1,0:T(2,128)}) custom-call(s32[32]{0:T(128)} %owner_ref.1, s32[2,64]{1,0:T(2,128)} %bitcast.11, f32[4,33]{1,0:T(4,128)} %taps_ref.1, s32[1,64]{1,0:T(1,128)} %bitcast.12, f32[2,512]{1,0:T(2,128)} %gains_ref.1, bf16[2,4,256,2048]{3,2,1,0:T(8,128)(2,1)} %bitcast.7, ...), custom_call_target="tpu_custom_call" | custom-call | tf_op jit(solution)/shard_map/sky_to_residual/pallas_call | solution.py:535
  47.3 2.1 %handed_on.1 = (bf16[8,128,512]{2,1,0:T(8,128)(2,1)}, f32[128,2,128]{2,1,0:T(2,128)}) custom-call(bf16[8,128,512]{2,1,0:T(8,128)(2,1)} %bitcast.10, f32[128,2,128]{2,1,0:T(2,128)} %get-tuple-element.7.b_ref), custom_call_target="tpu_custom_call" | custom-call | tf_op jit(solution)/shard_map/handed_on/pallas_call | solution.py:483

commit v5 on v3

--- a/solution.py
+++ b/solution.py
@@ -95,9 +95,9 @@
     fcols_in,
     offset_in,
     index_in,
-    observed_in,
     subgrid_out,
-    residual_out,
+    arrived,
+    product_out,
     x_buf,
     col_taper,
     row_taper,
@@ -105,7 +105,6 @@
     fcols,
     offsets,
     index,
-    observed,
     pad_ref,
     across_ref,
     down_ref,
@@ -124,8 +123,6 @@
     onehot,
     values,
     outgoing,
-    arrived,
-    wide,
     product,
     load_sem,
     strip_send,
@@ -136,6 +133,7 @@
     vis_recv,
     out_sem,
     ready_sem,
+    wave_sem,
 ):
     corr, scales, rows, side = x_ref.shape
     width = (taps_ref.shape[1] - 1) // 2
@@ -148,7 +146,7 @@
     blocks = offsets.shape[0]
     vis = offsets.shape[2]
     devices = n_facet * n_strip
-    capacity = observed.shape[0] // devices
+    capacity = outgoing.shape[1] // corr
     sub_cols = col_taper.shape[0]
     sub_rows = row_taper.shape[0]
     r_blocks, q_blocks = sub_side // LANES, sub_side // ALIGN
@@ -175,14 +173,13 @@
                 (offset_in, offsets),
                 (frows_in, frows),
                 (fcols_in, fcols),
-                (observed_in, observed),
             )
         )
     ]
-    index_load, offset_load, frows_load, fcols_load, observed_load = others
+    index_load, offset_load, frows_load, fcols_load = others
     col_loads = [
         pltpu.make_async_copy(
-            col_in.at[:, pl.ds(b * contrib, contrib)], col_taper.at[b], load_sem.at[corr * n_chunk + 5 + b]
+            col_in.at[:, pl.ds(b * contrib, contrib)], col_taper.at[b], load_sem.at[corr * n_chunk + 4 + b]
         )
         for b in range(sub_cols)
     ]
@@ -190,7 +187,7 @@
         pltpu.make_async_copy(
             row_in.at[:, pl.ds(a * contrib, contrib)],
             row_taper.at[a],
-            load_sem.at[corr * n_chunk + 5 + sub_cols + a],
+            load_sem.at[corr * n_chunk + 4 + sub_cols + a],
         )
         for a in range(sub_rows)
     ]
@@ -202,10 +199,18 @@
         pl.semaphore_signal(
             barrier, inc=1, device_id={"strip": lax.rem(s_me + off, n_strip)}, device_id_type=MESH
         )
-    for off in range(1, n_facet):
-        pl.semaphore_signal(
-            barrier, inc=1, device_id={"facet": lax.rem(f_me + off, n_facet)}, device_id_type=MESH
-        )
+    near = jnp.minimum(f_me, 1) + jnp.minimum(n_facet - 1 - f_me, 1)
+
+    def signal_near(sem):
+        @pl.when(f_me > 0)
+        def _():
+            pl.semaphore_signal(sem, inc=1, device_id={"facet": f_me - 1}, device_id_type=MESH)
+
+        @pl.when(f_me < n_facet - 1)
+        def _():
+            pl.semaphore_signal(sem, inc=1, device_id={"facet": f_me + 1}, device_id_type=MESH)
+
+    signal_near(barrier)
     fill_bands(taps_ref, pad_ref, across_ref, down_ref, width, chunks)
     y_ref[:, :, 0:LANES] = jnp.zeros((scales, tall, LANES), y_ref.dtype)
     y_ref[:, :, LANES + side : 2 * LANES + side] = jnp.zeros((scales, tall, LANES), y_ref.dtype)
@@ -235,14 +240,8 @@
         if n_part == 0:
             for load in col_loads:
                 load.wait()
-            pl.semaphore_wait(barrier, n_strip + n_facet - 2)
-            for off in range(1, n_strip):
-                pl.semaphore_signal(
-                    ready_sem,
-                    inc=1,
-                    device_id={"strip": lax.rem(s_me + off, n_strip)},
-                    device_id_type=MESH,
-                )
+            pl.semaphore_wait(barrier, n_strip - 1 + near)
+            signal_near(wave_sem.at[0])
         for first in range(1, n_strip + 1, 2):
             peers = [lax.rem(s_me + off, n_strip) for off in (first, first + 1)]
             pair = jnp.concatenate([col_taper[position_of(col_perm, peer)] for peer in peers], axis=1)
@@ -264,6 +263,18 @@
                 )
                 copy.start()
                 strip_copies.append(copy)
+        if n_part == 0:
+            continue
+        last = n_part == corr * n_chunk - 1
+        for wave in range(n_part - 1, n_facet - 2 if last else n_part):
+            if wave < n_facet - 2:
+                pl.semaphore_wait(wave_sem.at[wave], near)
+            if wave + 1 < n_facet - 2:
+                signal_near(wave_sem.at[wave + 1])
+    for off in range(1, n_strip):
+        pl.semaphore_signal(
+            ready_sem, inc=1, device_id={"strip": lax.rem(s_me + off, n_strip)}, device_id_type=MESH
+        )
 
     turned[:, r_blocks] = jnp.zeros((corr,) + turned.shape[2:], turned.dtype)
     turned[:, :, q_blocks] = jnp.zeros((corr, r_blocks + 1, ALIGN, LANES), turned.dtype)
@@ -372,13 +383,15 @@
             values[pl.ds(c * blocks + k, 1), :] = jnp.sum(along * col_weights[k], axis=0, keepdims=True)
             return carry
 
-        lax.fori_loop(0, blocks, one_block, 0, unroll=8)
+        lax.fori_loop(0, blocks, one_block, 0, unroll=16)
 
     contribute(0)
     index_load.wait()
     for n in range(corr):
         row = gains_ref[n : n + 1, :]
         product[n] = looked_up(row, index[:, 0, :]) * looked_up(row, index[:, 1, :])
+    product_copy = pltpu.make_async_copy(product, product_out, out_sem.at[corr])
+    product_copy.start()
     dest = dest_ref[...]
     k_row = lax.broadcasted_iota(jnp.int32, (blocks, blocks), 0)
     k_col = lax.broadcasted_iota(jnp.int32, (blocks, blocks), 1)
@@ -420,8 +433,9 @@
             )
             copy.start()
             vis_copies.append(copy)
-    arrived[me] = outgoing[me]
-    subgrid_copies = []
+    own_copy = pltpu.make_async_copy(outgoing.at[me], arrived.at[me], out_sem.at[corr + 1])
+    own_copy.start()
+    subgrid_copies = [product_copy, own_copy]
     for c in range(corr):
         subgrid[c] = lax.dot_general(
             row_mats[...], spread[c], ACROSS, preferred_element_type=jnp.float32
@@ -429,53 +443,70 @@
         copy = pltpu.make_async_copy(subgrid.at[c], subgrid_out.at[c], out_sem.at[c])
         copy.start()
         subgrid_copies.append(copy)
-    observed_load.wait()
 
     for copy in vis_copies:
         copy.wait()
+    for copy in subgrid_copies:
+        copy.wait()
+
+
+def close_kernel(
+    subgrid_in, arrived_in, product_in, observed_in, subgrid_out, residual_out,
+    subgrid, arrived, product, observed, residual, wide, in_sem, out_sem,
+):
+    parts = subgrid_in.shape[0]
+    corr, slots = product.shape[:2]
+    small = ((arrived_in, arrived), (product_in, product), (observed_in, observed))
+    loads = [
+        pltpu.make_async_copy(src, dst, in_sem.at[parts + n]) for n, (src, dst) in enumerate(small)
+    ]
+    cut_loads = [
+        pltpu.make_async_copy(subgrid_in.at[n], subgrid.at[n], in_sem.at[n]) for n in range(parts)
+    ]
+    stores = [
+        pltpu.make_async_copy(subgrid.at[n], subgrid_out.at[n], out_sem.at[n]) for n in range(parts)
+    ]
+    for load in loads + cut_loads:
+        load.start()
+    for load in loads:
+        load.wait()
     wide[...] = arrived[...].astype(jnp.float32).reshape(wide.shape)
     for c in range(corr):
-        placed = wide[pl.ds(c, devices * capacity, stride=corr), :]
-        residual_out[:, c, :] = observed[:, c, :] - product[c] * placed
-    for copy in subgrid_copies:
-        copy.wait()
-
-
-def pass_kernel(a_ref, b_ref, a_out, b_out, a_buf, b_buf, in_sem, out_sem):
-    parts = a_ref.shape[0]
-    pairs = [(a_ref.at[n], a_buf.at[n], a_out.at[n]) for n in range(parts)]
-    pairs.append((b_ref, b_buf, b_out))
-    loads = [pltpu.make_async_copy(src, buf, in_sem.at[n]) for n, (src, buf, _) in enumerate(pairs)]
-    stores = [pltpu.make_async_copy(buf, dst, out_sem.at[n]) for n, (_, buf, dst) in enumerate(pairs)]
-    for load in loads:
-        load.start()
-    for load, store in zip(loads, stores):
+        placed = wide[pl.ds(c, slots, stride=corr), :]
+        residual[:, c, :] = observed[:, c, :] - product[c] * placed
+    stores.append(pltpu.make_async_copy(residual, residual_out, out_sem.at[parts]))
+    stores[-1].start()
+    for load, store in zip(cut_loads, stores):
         load.wait()
         store.start()
     for store in stores:
         store.wait()
 
 
-def handed_on(subgrid, residual):
-    parts = 8
+def closed(subgrid, arrived, product, observed):
+    parts = 4
     cut = subgrid.reshape(parts, -1, subgrid.shape[-1])
     remote = pl.BlockSpec(memory_space=pl.ANY)
     a, b = pl.pallas_call(
-        pass_kernel,
-        in_specs=[remote, remote],
+        close_kernel,
+        in_specs=[remote] * 4,
         out_specs=[remote, remote],
         out_shape=[
             jax.ShapeDtypeStruct(cut.shape, cut.dtype),
-            jax.ShapeDtypeStruct(residual.shape, residual.dtype),
+            jax.ShapeDtypeStruct(observed.shape, observed.dtype),
         ],
         scratch_shapes=[
             pltpu.VMEM(cut.shape, cut.dtype),
-            pltpu.VMEM(residual.shape, residual.dtype),
-            pltpu.SemaphoreType.DMA((parts + 1,)),
+            pltpu.VMEM(arrived.shape, arrived.dtype),
+            pltpu.VMEM(product.shape, product.dtype),
+            pltpu.VMEM(observed.shape, observed.dtype),
+            pltpu.VMEM(observed.shape, observed.dtype),
+            pltpu.VMEM((arrived.shape[0] * arrived.shape[1], arrived.shape[2]), jnp.float32),
+            pltpu.SemaphoreType.DMA((parts + 3,)),
             pltpu.SemaphoreType.DMA((parts + 1,)),
         ],
-        name="handed_on",
-    )(cut, residual)
+        name="closed",
+    )(cut, arrived, product, observed)
     return a.reshape(subgrid.shape), b
 
 
@@ -512,13 +543,14 @@
     remote = pl.BlockSpec(memory_space=pl.ANY)
     bf16, f32 = jnp.bfloat16, jnp.float32
     dma = pltpu.SemaphoreType.DMA
-    subgrid, residual = pl.pallas_call(
+    subgrid, arrived, product = pl.pallas_call(
         functools.partial(whole_kernel, n_facet, n_strip),
-        in_specs=[scalars, scalars, whole, whole, whole] + [remote] * 8,
-        out_specs=[remote, whole],
+        in_specs=[scalars, scalars, whole, whole, whole] + [remote] * 7,
+        out_specs=[remote] * 3,
         out_shape=[
             jax.ShapeDtypeStruct((corr, sub_side, sub_side), bf16),
-            jax.ShapeDtypeStruct(observed.shape, f32),
+            jax.ShapeDtypeStruct((devices, per_device, vis), bf16),
+            jax.ShapeDtypeStruct((corr, slots, vis), f32),
         ],
         scratch_shapes=[
             pltpu.VMEM((corr, scales, rows, side), bf16),
@@ -528,7 +560,6 @@
             pltpu.VMEM(finish_cols.shape, bf16),
             pltpu.VMEM(vis_offset.shape, f32),
             pltpu.VMEM(antenna_pair_index.shape, jnp.int32),
-            pltpu.VMEM(observed.shape, f32),
             pltpu.VMEM((scales, 2 * LANES), f32),
             pltpu.VMEM((n_chunk, scales, tall, chunks[0][3] - chunks[0][2]), bf16),
             pltpu.VMEM((scales, COL_TILE + 2 * LANES, COL_TILE), bf16),
@@ -547,18 +578,17 @@
             pltpu.VMEM((devices * per_device, corr * blocks), bf16),
             pltpu.VMEM((corr * blocks, vis), f32),
             pltpu.VMEM((devices, per_device, vis), bf16),
-            pltpu.VMEM((devices, per_device, vis), bf16),
-            pltpu.VMEM((devices * per_device, vis), f32),
             pltpu.VMEM((corr, slots, vis), f32),
-            dma((corr * n_chunk + 5 + sub_cols + sub_rows,)),
+            dma((corr * n_chunk + 4 + sub_cols + sub_rows,)),
             dma((corr * n_chunk, n_strip)),
             dma((corr * n_chunk, n_strip)),
             dma((corr, n_facet)),
             dma((corr, n_facet)),
             dma((devices,)),
             dma((devices,)),
-            dma((corr,)),
+            dma((corr + 2,)),
             pltpu.SemaphoreType.REGULAR,
+            pltpu.SemaphoreType.REGULAR((max(n_facet - 2, 1),)),
         ],
         compiler_params=pltpu.CompilerParams(
             collective_id=0, has_side_effects=True, vmem_limit_bytes=60 * 1024 * 1024
@@ -577,9 +607,8 @@
         finish_cols,
         vis_offset,
         antenna_pair_index,
-        observed,
     )
-    subgrid, residual = handed_on(subgrid, residual)
+    subgrid, residual = closed(subgrid, arrived, product, observed)
     return subgrid[None], residual
 
 

time: 48.3 us -> 47.2 us (0.977)
  Pallas kernels: 47.3 us -> 46.2 us
    pallas_call x1, Pallas kernels: 45.1 us -> 44 us  [on_device(): pl.pallas_call(functools.partial(whole_kernel, n_facet, n_strip), in_spec...]
where the time goes in v5:
time: 47.2 us; the launch traced here: 47 us
  Pallas kernels  46.2 us (98%)
  between operations  0.8 us (2%)
    pallas_call x1, Pallas kernels, on_device(): pl.pallas_call(functools.partial(whole_kernel, n_facet, n_strip), in_spec...  44 us
    pallas_call x1, Pallas kernels, closed(): pl.pallas_call(close_kernel, in_specs=[remote] * 4, out_specs=[remote, re...  2.28 us

profile of v5, /device:TPU:0, one launch (start us, length us, event | category | flops | bytes accessed | tf_op | source)
XLA Modules:
  0.0 47.0 jit_solution(3849614322934859744)
XLA Ops:
  0.6 44.0 %sky_to_residual.1 = (bf16[2,512,512]{2,1,0:T(8,128)(2,1)}, bf16[32,8,128]{2,1,0:T(8,128)(2,1)}, f32[2,128,128]{2,1,0:T(8,128)}) custom-call(s32[32]{0:T(128)} %owner_ref.1, s32[2,64]{1,0:T(2,128)} %bitcast.11, f32[4,33]{1,0:T(4,128)} %taps_ref.1, s32[1,64]{1,0:T(1,128)} %bitcast.12, f32[2,512]{1,0:T(2,128)} %gains_ref.1, bf16[2,4,256,2048]{3,2,1,0:T(8,128)(2,1)} %bitcast.7, ...), custom_call_target="tpu_custom_call" | custom-call | tf_op jit(solution)/shard_map/sky_to_residual/pallas_call | solution.py:546
  44.6 2.3 %closed.1 = (bf16[4,256,512]{2,1,0:T(8,128)(2,1)}, f32[128,2,128]{2,1,0:T(2,128)}) custom-call(bf16[4,256,512]{2,1,0:T(8,128)(2,1)} %bitcast.10, bf16[32,8,128]{2,1,0:T(8,128)(2,1)} %get-tuple-element.8.arrived_in, f32[2,128,128]{2,1,0:T(8,128)} %get-tuple-element.9.product_in, f32[128,2,128]{2,1,0:T(2,128)} %observed_in.1), custom_call_target="tpu_custom_call" | custom-call | tf_op jit(solution)/shard_map/closed/pallas_call | solution.py:490

commit v6 on v5

--- a/solution.py
+++ b/solution.py
@@ -11,6 +11,7 @@
 KERNEL_WIDTH = 1.5
 LANES = 128
 COL_TILE = 256
+BAND = COL_TILE + LANES
 ALIGN = 16
 TALL = TILE + ALIGN
 WIDE = LANES + TILE
@@ -23,11 +24,12 @@
 
 
 def row_chunks(rows, width):
-    count = rows // LANES
+    count = max(1, rows // COL_TILE)
+    step = rows // count
     chunks = []
     for h in range(count):
-        low = h * LANES if h else -width
-        high = (h + 1) * LANES if h < count - 1 else rows + width
+        low = h * step if h else -width
+        high = (h + 1) * step if h < count - 1 else rows + width
         chunks.append((low, high, max(0, low - width), min(rows, high + width)))
     return chunks
 
@@ -39,7 +41,7 @@
     pad_ref[:, 0:taps] = taps_ref[...]
     down_ref[...] = jnp.zeros_like(down_ref)
     for s in range(scales):
-        row = jnp.broadcast_to(pad_ref[s : s + 1, :], (LANES, 2 * LANES))
+        row = jnp.broadcast_to(pad_ref[s : s + 1, 0 : 2 * LANES], (LANES, 2 * LANES))
         band = pltpu.roll(row, 0, 1, stride=1, stride_axis=0)
         down = band.T[:span].astype(down_ref.dtype)
         for tile in range(COL_TILE // LANES):
@@ -48,8 +50,8 @@
         for h, (low, high, x_low, x_high) in enumerate(chunks):
             for first in range(0, high - low, LANES):
                 size = min(LANES, high - low - first)
-                line = jnp.broadcast_to(pad_ref[s : s + 1, :], (size, 2 * LANES))
-                shift = (low - width - x_low + first) % (2 * LANES)
+                line = jnp.broadcast_to(pad_ref[s : s + 1, :], (size, BAND))
+                shift = (low - width - x_low + first) % BAND
                 if shift:
                     line = pltpu.roll(line, shift, 1)
                 line = pltpu.roll(line, 0, 1, stride=1, stride_axis=0)
@@ -236,7 +238,7 @@
             smooth_ref[:, pl.ds(first, COL_TILE)] = smoothed.astype(smooth_ref.dtype)
             return carry
 
-        lax.fori_loop(0, tiles, one_tile, 0, unroll=4)
+        lax.fori_loop(0, tiles, one_tile, 0, unroll=2)
         if n_part == 0:
             for load in col_loads:
                 load.wait()
@@ -560,7 +562,7 @@
             pltpu.VMEM(finish_cols.shape, bf16),
             pltpu.VMEM(vis_offset.shape, f32),
             pltpu.VMEM(antenna_pair_index.shape, jnp.int32),
-            pltpu.VMEM((scales, 2 * LANES), f32),
+            pltpu.VMEM((scales, BAND), f32),
             pltpu.VMEM((n_chunk, scales, tall, chunks[0][3] - chunks[0][2]), bf16),
             pltpu.VMEM((scales, COL_TILE + 2 * LANES, COL_TILE), bf16),
             pltpu.VMEM((scales, tall, side + 2 * LANES), bf16),

time: 47.2 us -> 47.1 us (level)
  no operation moved by 1% of the time
where the time goes in v6:
time: 47.1 us; the launch traced here: 46.9 us
  Pallas kernels  46.1 us (98%)
  between operations  0.8 us (2%)
    pallas_call x1, Pallas kernels, on_device(): pl.pallas_call(functools.partial(whole_kernel, n_facet, n_strip), in_spec...  43.8 us
    pallas_call x1, Pallas kernels, closed(): pl.pallas_call(close_kernel, in_specs=[remote] * 4, out_specs=[remote, re...  2.28 us

profile of v6, /device:TPU:0, one launch (start us, length us, event | category | flops | bytes accessed | tf_op | source)
XLA Modules:
  0.0 46.9 jit_solution(17866468350070354928)
XLA Ops:
  0.6 43.8 %sky_to_residual.1 = (bf16[2,512,512]{2,1,0:T(8,128)(2,1)}, bf16[32,8,128]{2,1,0:T(8,128)(2,1)}, f32[2,128,128]{2,1,0:T(8,128)}) custom-call(s32[32]{0:T(128)} %owner_ref.1, s32[2,64]{1,0:T(2,128)} %bitcast.11, f32[4,33]{1,0:T(4,128)} %taps_ref.1, s32[1,64]{1,0:T(1,128)} %bitcast.12, f32[2,512]{1,0:T(2,128)} %gains_ref.1, bf16[2,4,256,2048]{3,2,1,0:T(8,128)(2,1)} %bitcast.7, ...), custom_call_target="tpu_custom_call" | custom-call | tf_op jit(solution)/shard_map/sky_to_residual/pallas_call | solution.py:548
  44.4 2.3 %closed.1 = (bf16[4,256,512]{2,1,0:T(8,128)(2,1)}, f32[128,2,128]{2,1,0:T(2,128)}) custom-call(bf16[4,256,512]{2,1,0:T(8,128)(2,1)} %bitcast.10, bf16[32,8,128]{2,1,0:T(8,128)(2,1)} %get-tuple-element.8.arrived_in, f32[2,128,128]{2,1,0:T(8,128)} %get-tuple-element.9.product_in, f32[128,2,128]{2,1,0:T(2,128)} %observed_in.1), custom_call_target="tpu_custom_call" | custom-call | tf_op jit(solution)/shard_map/closed/pallas_call | solution.py:492
